TPU v7x, 256 devices: a whole 4x4x8 slice. The times are simulated.
256 devices in a mesh: ia: 16 (over x_hi, z), ja: 8 (over x_lo, y), row: 2 (over core).
Axes of the slice: x: 4 (x_hi: 2, x_lo: 2; x = x_hi * 2 + x_lo), y: 4, z: 8, core: 2. Of those that a mesh axis runs over, the one named last changes fastest.
Arguments:
- amplitudes: float32 [16, 16, 1024, 1024], P('ia', ('ja', 'row')), may hold values from -6 to 6
- cycle_inter: float32 [2, 16, 1024, 1024], P(None, ('ja', 'row'), 'ia'), may hold values from -0.125 to 0.125
- occ_energy: float32 [256], replicated, may hold values from -2 to -0.3
- virt_energy: float32 [1024], replicated, may hold values from 0.3 to 3
- window_orbs: int32 [16], replicated, may hold values from 0 to 255, as said below
- internal_pos: int32 [2], replicated, may hold values from 0 to 15, as said below
- virt_order: int32 [1024], replicated, may hold values from 0 to 1023, each once
Outputs:
- updated: float32 [16, 16, 1024, 1024], P('ia', ('ja', 'row'))
Inputs may be any that keep to these rules, and one draw needn't show every extreme that they name: `window_orbs`: 16 distinct orbital numbers. `internal_pos`: 2 distinct window positions, one of which is the last position 15.
All inputs are finite; a program needn't handle non-finite values.
Results may differ from a plain program's by a relative error of at most 0.00005.
Values sent between devices are 32-bit elements; how exact they have to be, the bound alone decides.
No kernel may reach another device: no remote copies, remote signals or barrier semaphores. Data moves between devices by JAX's collectives and lax.ppermute only.
A program may use at most 128 MiB of HBM per device.

v0:
```python
import functools

import jax
import jax.numpy as jnp
from jax import lax
from jax.experimental import pallas as pl
from jax.experimental.pallas import tpu as pltpu
from jax.sharding import PartitionSpec as P


AXES = ("ia", "ja", "row")
NXH, NZ, NXL, NY, NC = 2, 8, 2, 4, 2
F32, BF16 = jnp.float32, jnp.bfloat16


def place(xh, z, xl, y, c):
    return ((xh * NZ + z) * NXL * NY + xl * NY + y) * NC + c


def permute(array, target, sends=None):
    pairs = []
    for xh in range(NXH):
        for z in range(NZ):
            for xl in range(NXL):
                for y in range(NY):
                    for c in range(NC):
                        at = (xh, z, xl, y, c)
                        if sends is None or sends(*at):
                            pairs.append((place(*at), place(*target(*at))))
    return lax.ppermute(array, AXES, pairs)


TURNS = (0, 2, 1, 3)


def swap_core(xh, z, xl, y, c):
    return xh, z, xl, y, 1 - c


def swap_xl(xh, z, xl, y, c):
    return xh, z, 1 - xl, y, c


def swap_xh(xh, z, xl, y, c):
    return 1 - xh, z, xl, y, c


def shift_y(step):
    return lambda xh, z, xl, y, c: (xh, z, xl, (y + step) % NY, c)


def shift_z(step):
    return lambda xh, z, xl, y, c: (xh, (z + step) % NZ, xl, y, c)


LATE = (3,)


def mirror_z(n):
    def to(xh, z, xl, y, c):
        xh, xl = (xh, xl) if n in LATE else (xl, xh)
        return xh, 2 * ((z // 2 - n - y) % NY) + c, xl, y, z % 2

    return to


def mirror_y(n):
    def to(xh, z, xl, y, c):
        xh, xl = (xl, xh) if n in LATE else (xh, xl)
        return xh, z, xl, (z // 2 + n + y) % NY, c

    return to


def home_y(n):
    return lambda xh, z, xl, y, c: (xh, z, xl, (z // 2 - n - y) % NY, c)


def form_kernel(s_ref, rows_own, cols_own, rows_got, cols_got, *outs):
    own = s_ref[5] != 0
    rows = jnp.where(own, rows_own[...], rows_got[...])
    cols = jnp.where(own, cols_own[...], cols_got[...])
    value = 2.0 * rows - cols.T
    for i, out in enumerate(outs):

        @pl.when(pl.program_id(0) == i)
        def _():
            out[...] = value


def form_own_kernel(s_ref, rows, cols, *outs):
    value = 2.0 * rows[...] - cols[...].T
    for i, out in enumerate(outs):

        @pl.when(pl.program_id(0) == i)
        def _():
            out[pl.program_id(1)] = value


def form_own(tile, scal):
    v = tile.shape[0]
    tb = v // (2 * NY)
    at = lambda g, half, s: half * NY + (s[3] + g) % NY
    return pl.pallas_call(
        form_own_kernel,
        grid_spec=pltpu.PrefetchScalarGridSpec(
            num_scalar_prefetch=1,
            grid=(NY, 2),
            in_specs=[
                pl.BlockSpec((tb, v), lambda g, h, s: (at(g, h, s), 0)),
                pl.BlockSpec((v, tb), lambda g, h, s: (0, at(g, h, s))),
            ],
            out_specs=[pl.BlockSpec((2, tb, v), lambda g, h, s: (0, 0, 0))] * NY,
        ),
        out_shape=[jax.ShapeDtypeStruct((2, tb, v), F32)] * NY,
        name="form_own",
        compiler_params=pltpu.CompilerParams(vmem_limit_bytes=24 * 2**20),
    )(scal, tile, tile)


def form(tile, got, scal):
    v = tile.shape[0]
    tb = v // (2 * NY)
    at = lambda g, s: s[4] * NY + (s[3] + g) % NY
    ins = [
        pl.BlockSpec((tb, v), lambda g, s: (at(g, s), 0)),
        pl.BlockSpec((v, tb), lambda g, s: (0, at(g, s))),
    ]
    return pl.pallas_call(
        form_kernel,
        grid_spec=pltpu.PrefetchScalarGridSpec(
            num_scalar_prefetch=1,
            grid=(NY,),
            in_specs=ins + ins,
            out_specs=[pl.BlockSpec((tb, v), lambda g, s: (0, 0))] * NY,
        ),
        out_shape=[jax.ShapeDtypeStruct((tb, v), F32)] * NY,
        name="form",
        compiler_params=pltpu.CompilerParams(vmem_limit_bytes=24 * 2**20),
    )(scal, tile, tile, got, got)


def split(value):
    high = value.astype(BF16)
    return high, (value - high.astype(F32)).astype(BF16)


def lay_kernel(s_ref, own, got, high_ref, low_ref):
    c = s_ref[4]
    for core, src in ((c, own), (1 - c, got)):
        high, low = split(src[0])
        high_ref[core, 0] = high
        low_ref[core, 0] = low


def lay(own, got, scal):
    _, rows, v = own.shape
    spec = pl.BlockSpec((1, rows, v), lambda g, s: (g, 0, 0))
    out = pl.BlockSpec((2, 1, rows, v), lambda g, s: (0, (s[3] + NY - g) % NY, 0, 0))
    shape = jax.ShapeDtypeStruct((2, NY, rows, v), BF16)
    high, low = pl.pallas_call(
        lay_kernel,
        grid_spec=pltpu.PrefetchScalarGridSpec(
            num_scalar_prefetch=1,
            grid=(NY,),
            in_specs=[spec] * 2,
            out_specs=[out] * 2,
        ),
        out_shape=[shape] * 2,
        name="lay",
        compiler_params=pltpu.CompilerParams(vmem_limit_bytes=24 * 2**20),
    )(scal, own, got)
    return high.reshape(v, v), low.reshape(v, v)


def product_kernel(where, count, s_ref, *refs):
    tiles, refs = refs[:4], refs[4:]
    chunks, refs = refs[: count * len(where)], refs[count * len(where) :]
    outs, scratch = refs[:count], refs[count:]

    @pl.when(pl.program_id(0) == 0)
    def _():
        for i, chunk in enumerate(chunks):
            other, dz = where[i % len(where)]
            w_high, w_low = scratch[2 * (i // len(where))], scratch[2 * (i // len(where)) + 1]
            xh = jnp.where(other, 1 - s_ref[0], s_ref[0])
            z = (s_ref[1] + dz + NZ) % NZ
            _, two, depth, _ = chunk.shape
            for k in range(two):
                at = ((k * NXH + xh) * NZ + z) * depth
                rows = pl.ds(pl.multiple_of(at, depth), depth)
                high, low = split(chunk[0, k])
                w_high[rows, :] = high
                w_low[rows, :] = low

    dot = functools.partial(jnp.dot, preferred_element_type=F32)
    for i, out in enumerate(outs):
        w_high, w_low = scratch[2 * i], scratch[2 * i + 1]
        total = 0.0
        for k in range(2):
            high, low = tiles[2 * k][...], tiles[2 * k + 1][...]
            rows = slice(k * high.shape[1], (k + 1) * high.shape[1])
            total += dot(high, w_high[rows, :])
            total += dot(high, w_low[rows, :]) + dot(low, w_high[rows, :])
        out[...] = total


def product(tiles, chunks, where, ns, scal):
    v = tiles[0].shape[0]
    depth = 2 * v
    _, two, rows, cols = chunks[0].shape
    steps = 4
    tb = v // steps
    xs = pl.BlockSpec((tb, v), lambda g, s: (g, 0))
    ws = lambda n: pl.BlockSpec(
        (1, two, rows, cols),
        lambda g, s: ((2 * s[3] + NY - s[1] // 2 + n) % NY, 0, 0, 0),
    )
    return pl.pallas_call(
        functools.partial(product_kernel, where, len(ns)),
        grid_spec=pltpu.PrefetchScalarGridSpec(
            num_scalar_prefetch=1,
            grid=(steps,),
            in_specs=[xs] * 4 + [ws(n) for n in ns for _ in chunks],
            out_specs=[pl.BlockSpec((tb, cols), lambda g, s: (g, 0))] * len(ns),
            scratch_shapes=[pltpu.VMEM((depth, cols), BF16)] * (2 * len(ns)),
        ),
        out_shape=[jax.ShapeDtypeStruct((v, cols), F32)] * len(ns),
        cost_estimate=pl.CostEstimate(
            flops=6 * v * depth * cols * len(ns),
            bytes_accessed=12 * 2**20,
            transcendentals=0,
        ),
        name="product",
        compiler_params=pltpu.CompilerParams(vmem_limit_bytes=28 * 2**20),
    )(scal, *tiles, *(chunks * len(ns)))


def begin_kernel(s_ref, tile, e_pair, e_row, e_col, *refs):
    direct, out, inverse = refs[:4], refs[4], refs[5]
    w = direct[0].shape[1]
    for n in range(4):
        at = pl.ds(pl.multiple_of(((s_ref[1] // 2 + 2 * NY - n - s_ref[3]) % NY) * w, w), w)
        inv = 1.0 / ((e_pair[0, 0] - e_col[...]) - e_row[:, at])
        inverse[:, at] = inv
        out[:, at] = tile[:, at] + direct[n][...] * inv


def begin(tile, e_pair, e_virt, direct, scal):
    v, w = tile.shape[0], direct[0].shape[1]
    steps = 4
    row = lambda width: pl.BlockSpec((v // steps, width), lambda g, s: (g, 0))
    return pl.pallas_call(
        begin_kernel,
        grid_spec=pltpu.PrefetchScalarGridSpec(
            num_scalar_prefetch=1,
            grid=(steps,),
            in_specs=[
                row(v),
                pl.BlockSpec(memory_space=pltpu.SMEM),
                pl.BlockSpec((1, v), lambda g, s: (0, 0)),
                row(1),
            ]
            + [row(w)] * 4,
            out_specs=[row(v)] * 2,
        ),
        out_shape=[jax.ShapeDtypeStruct((v, v), F32)] * 2,
        name="begin",
        compiler_params=pltpu.CompilerParams(vmem_limit_bytes=24 * 2**20),
    )(scal, tile, e_pair, e_virt[None, :], e_virt[:, None], *direct)


def finish_kernel(s_ref, total, inverse, mirror, out):
    out[...] = total[...] + mirror[...].T * inverse[...]


def finish(n, total, inverse, mirror, scal):
    v, w = mirror.shape
    steps = 4
    at = lambda s: (s[3] + 2 * NY - s[1] // 2 - n) % NY
    block = pl.BlockSpec((w, v // steps), lambda g, s: (at(s), g))
    return pl.pallas_call(
        finish_kernel,
        grid_spec=pltpu.PrefetchScalarGridSpec(
            num_scalar_prefetch=1,
            grid=(steps,),
            in_specs=[block, block, pl.BlockSpec((v // steps, w), lambda g, s: (g, 0))],
            out_specs=block,
        ),
        out_shape=jax.ShapeDtypeStruct((v, v), F32),
        input_output_aliases={1: 0},
        name="finish",
        compiler_params=pltpu.CompilerParams(vmem_limit_bytes=24 * 2**20),
    )(scal, total, inverse, mirror)


def pick(index, arrays):
    result = arrays[0]
    for i in range(1, len(arrays)):
        result = jnp.where(index == i, arrays[i], result)
    return result


def step(
    amplitudes, cycle_inter, occ_energy, virt_energy, window_orbs, internal_pos, virt_order
):
    tile = amplitudes[0, 0]
    v = tile.shape[0]
    last = lax.axis_size("ja") * lax.axis_size("row") - 1
    ia, ja, c = lax.axis_index("ia"), lax.axis_index("ja"), lax.axis_index("row")
    xh, z, xl, y = ia // NZ, ia % NZ, ja // NY, ja % NY
    a_first = internal_pos[0] == last
    other = jnp.where(a_first, internal_pos[1], internal_pos[0])
    b_xl, b_at, b_c = other // (NY * NC), (other // NC) % NY, other % NC
    scal = jnp.stack(
        [xh, z, xl, y, c, (c == b_c).astype(jnp.int32)]
    ).astype(jnp.int32)

    w = cycle_inter[:, 0]
    w = jnp.where(a_first, w, w[::-1])
    cols = v // NY
    part = lambda i: lax.dynamic_slice_in_dim(w, ((y + i) % NY) * cols, cols, 2)
    own = jnp.stack([part(0)] + [permute(part(i), shift_y(i)) for i in range(1, NY)])
    across = permute(own, swap_xh)
    chunks, where = [], []
    for far, start in ((False, own), (True, across)):
        chunks.append(start)
        where.append((far, 0))
        up = down = start
        for step in range(1, 4):
            up = permute(up, shift_z(1))
            down = permute(down, shift_z(-1))
            chunks += [up, down]
            where += [(far, -step), (far, step)]
        chunks.append(permute(down, shift_z(-1)) if far else permute(up, shift_z(1)))
        where.append((far, 4))

    got = permute(tile, swap_core)
    cut_a = form_own(tile, scal)
    cut_b = form(tile, got, scal)
    last_core = (
        lambda xh, z, xl, y, c: xl == NXL - 1 and y == NY - 1 and c == NC - 1
    )
    a_got = [permute(cut_a[i], shift_y(i), last_core) for i in range(1, NY)]
    a_one = pick((y + 1) % NY, [cut_a[0]] + a_got)
    a_low = a_one[0]
    a_d = permute(a_low, swap_core, lambda xh, z, xl, y, c: c == NC - 1)
    a_one = jnp.where(c == NC - 1, a_one[1], a_d)
    a_x = permute(a_one, swap_xl, lambda xh, z, xl, y, c: xl == NXL - 1)
    a_two = jnp.where(xl == NXL - 1, a_one, a_x)
    a_all = jnp.stack([a_two] + [permute(a_two, shift_y(i)) for i in range(1, NY)])
    a_core = permute(a_all, swap_core)
    b_got = [permute(cut_b[i], shift_y(i)) for i in range(1, NY)]
    b_one = pick((y - b_at) % NY, [cut_b[0]] + b_got)
    b_x = permute(b_one, swap_xl)
    b_two = jnp.where(xl == b_xl, b_one, b_x)
    b_y = [b_two] + [permute(b_two, shift_y(i)) for i in range(1, NY)]
    b_all = jnp.stack(b_y)
    b_core = permute(b_all, swap_core)
    tiles = lay(a_all, a_core, scal)
    tiles += lay(b_all, b_core, scal)

    pieces = {}
    for ns in (TURNS[:2], TURNS[2:]):
        made = product(tiles, chunks, tuple(where), ns, scal)
        pieces.update(zip(ns, made))
    direct, mirror = [], []
    for n in range(NY):
        mirror.append(permute(permute(pieces[n], mirror_z(n)), mirror_y(n)))
        direct.append(permute(pieces[n], home_y(n)))

    hits = window_orbs[:, None] == jnp.arange(occ_energy.shape[0], dtype=jnp.int32)[None, :]
    e_window = jnp.sum(jnp.where(hits, occ_energy[None, :], 0.0), axis=1)
    e_virt = jnp.take(virt_energy, virt_order)
    e_pair = (e_window[ia] + e_window[ja * NC + c]).reshape(1, 1)
    total, inverse = begin(tile, e_pair, e_virt, direct, scal)
    for n in TURNS:
        total = finish(n, total, inverse, mirror[n], scal)
    return total[None, None]


def solution(mesh):
    placed = (
        P("ia", ("ja", "row"), None, None),
        P(None, ("ja", "row"), "ia", None),
        P(),
        P(),
        P(),
        P(),
        P(),
    )
    return jax.shard_map(
        step,
        mesh=mesh,
        in_specs=placed,
        out_specs=P("ia", ("ja", "row"), None, None),
        check_vma=False,
    )
```

profile of v0, /device:TPU:149, one launch (start us, length us, event | category | flops | bytes accessed | tf_op | source)
XLA Modules:
  0.0 404.4 jit_solution(15747712970187195380)
XLA Ops:
  4.2 2.2 copy-done.1
  6.4 4.3 %form_own.1 = (f32[2,128,1024]{2,1,0:T(8,128)S(1)}, f32[2,128,1024]{2,1,0:T(8,128)S(1)}, f32[2,128,1024]{2,1,0:T(8,128)S(1)}, f32[2,128,1024]{2,1,0:T(8,128)}) custom-call(s32[6]{0:T(128)S(1)} %stack.76.s_ref, f32[1024,1024]{1,0:T(8,128)S(1)} %bitcast.38, f32[1024,1024]{1,0:T(8,128)S(1)} %bitcast.39), custom_call_target="tpu_custom_call" | custom-call | tf_op jit(solution)/shard_map/form_own/pallas_call | solution.py:104
  18.2 2.7 collective-permute-start.3
  20.9 2.2 copy-done.2
  23.1 4.2 %form.1 = (f32[128,1024]{1,0:T(8,128)S(1)}, f32[128,1024]{1,0:T(8,128)S(1)}, f32[128,1024]{1,0:T(8,128)S(1)}, f32[128,1024]{1,0:T(8,128)S(1)}) custom-call(s32[6]{0:T(128)S(1)} %stack.76.s_ref, f32[1024,1024]{1,0:T(8,128)S(1)} %bitcast.40, f32[1024,1024]{1,0:T(8,128)S(1)} %bitcast.41, f32[1024,1024]{1,0:T(8,128)} %collective-permute-done.9.rows_got.cols_got, ...), custom_call_target="tpu_custom_call" | custom-call | tf_op jit(solution)/shard_map/form/pallas_call | solution.py:129
  33.4 8.0 %collective-permute-done.10 = f32[128,1024]{1,0:T(8,128)} collective-permute-done((f32[128,1024]{1,0:T(8,128)S(1)}, f32[128,1024]{1,0:T(8,128)}, u32[]{:S(2)}, u32[]{:S(2)}) %collective-permute-start.10) | collective-permute-done | bytes 524320 | tf_op jit(solution)/shard_map/ppermute | solution.py:30
  41.4 10.3 %collective-permute-start.19 = (f32[2,64,256]{2,1,0:T(8,128)S(1)}, f32[2,64,256]{2,1,0:T(8,128)S(1)}, u32[]{:S(2)}, u32[]{:S(2)}) collective-permute-start(f32[2,64,256]{2,1,0:T(8,128)S(1)} %get-tuple-element.43), channel_id=1, source_target_pairs={{0,4},{1,5},{2,6},{3,7},{4,0},{5,1},{6,2},{7,3},{8,12},{9,13},{10,... | collective-permute-start | bytes 393224 | tf_op jit(solution)/shard_map/ppermute | solution.py:30
  51.7 1.8 collective-permute-start.18
  55.5 33.7 %collective-permute-start.13 = (f32[128,1024]{1,0:T(8,128)S(1)}, f32[128,1024]{1,0:T(8,128)}, u32[]{:S(2)}, u32[]{:S(2)}) collective-permute-start(f32[128,1024]{1,0:T(8,128)S(1)} %select_select_fusion.1), channel_id=1, source_target_pairs={{0,8},{1,9},{2,10},{3,11},{4,12},{5,13},{6,14},{7,15},{8,0},{9,1},... | collective-permute-start | bytes 1572872 | tf_op jit(solution)/shard_map/ppermute | solution.py:30
  90.2 1.9 collective-permute-start.5
  92.8 3.3 collective-permute-done.13
  97.7 5.9 %collective-permute-start.15 = (f32[128,1024]{1,0:T(8,128)S(1)}, f32[128,1024]{1,0:T(8,128)S(1)}, u32[]{:S(2)}, u32[]{:S(2)}) collective-permute-start(f32[128,1024]{1,0:T(8,128)S(1)} %broadcast_select_fusion), channel_id=1, source_target_pairs={{0,4},{1,5},{2,6},{3,7},{4,0},{5,1},{6,2},{7,3},{8,12},{9,13},{10,... | collective-permute-start | bytes 1572872 | tf_op jit(solution)/shard_map/ppermute | solution.py:30
  109.4 2.1 collective-permute-done.15
  111.5 5.8 %collective-permute-done.14 = f32[128,1024]{1,0:T(8,128)S(1)} collective-permute-done((f32[128,1024]{1,0:T(8,128)S(1)}, f32[128,1024]{1,0:T(8,128)S(1)}, u32[]{:S(2)}, u32[]{:S(2)}) %collective-permute-start.14) | collective-permute-done | bytes 524320 | tf_op jit(solution)/shard_map/ppermute | solution.py:30
  118.4 5.4 %collective-permute-done.21.refs_5_.refs_21_ = f32[4,2,64,256]{3,2,1,0:T(8,128)S(1)} collective-permute-done((f32[4,2,64,256]{3,2,1,0:T(8,128)S(1)}, f32[4,2,64,256]{3,2,1,0:T(8,128)S(1)}, u32[]{:S(2)}, u32[]{:S(2)}) %collective-permute-start.21) | collective-permute-done | bytes 524320 | tf_op jit(solution)/shard_map/ppermute | solution.py:30
  126.1 8.9 %collective-permute-done.29.refs_13_.refs_29_ = f32[4,2,64,256]{3,2,1,0:T(8,128)S(1)} collective-permute-done((f32[4,2,64,256]{3,2,1,0:T(8,128)S(1)}, f32[4,2,64,256]{3,2,1,0:T(8,128)S(1)}, u32[]{:S(2)}, u32[]{:S(2)}) %collective-permute-start.29) | collective-permute-done | bytes 524320 | tf_op jit(solution)/shard_map/ppermute | solution.py:30
  135.1 2.6 collective-permute-done.24.refs_8_.refs_24_
  137.7 8.6 %collective-permute-done.23.refs_7_.refs_23_ = f32[4,2,64,256]{3,2,1,0:T(8,128)S(1)} collective-permute-done((f32[4,2,64,256]{3,2,1,0:T(8,128)S(1)}, f32[4,2,64,256]{3,2,1,0:T(8,128)S(1)}, u32[]{:S(2)}, u32[]{:S(2)}) %collective-permute-start.23) | collective-permute-done | bytes 524320 | tf_op jit(solution)/shard_map/ppermute | solution.py:30
  146.3 2.6 collective-permute-done.32.refs_16_.refs_32_
  149.9 7.6 %collective-permute-done.31.refs_15_.refs_31_ = f32[4,2,64,256]{3,2,1,0:T(8,128)S(1)} collective-permute-done((f32[4,2,64,256]{3,2,1,0:T(8,128)S(1)}, f32[4,2,64,256]{3,2,1,0:T(8,128)S(1)}, u32[]{:S(2)}, u32[]{:S(2)}) %collective-permute-start.31) | collective-permute-done | bytes 524320 | tf_op jit(solution)/shard_map/ppermute | solution.py:30
  157.5 10.6 %collective-permute-done.25.refs_9_.refs_25_ = f32[4,2,64,256]{3,2,1,0:T(8,128)S(1)} collective-permute-done((f32[4,2,64,256]{3,2,1,0:T(8,128)S(1)}, f32[4,2,64,256]{3,2,1,0:T(8,128)S(1)}, u32[]{:S(2)}, u32[]{:S(2)}) %collective-permute-start.25) | collective-permute-done | bytes 524320 | tf_op jit(solution)/shard_map/ppermute | solution.py:30
  168.7 2.4 collective-permute-start.35
  174.6 7.9 %collective-permute-done.33.refs_17_.refs_33_ = f32[4,2,64,256]{3,2,1,0:T(8,128)S(1)} collective-permute-done((f32[4,2,64,256]{3,2,1,0:T(8,128)S(1)}, f32[4,2,64,256]{3,2,1,0:T(8,128)S(1)}, u32[]{:S(2)}, u32[]{:S(2)}) %collective-permute-start.33) | collective-permute-done | bytes 524320 | tf_op jit(solution)/shard_map/ppermute | solution.py:30
  182.5 11.2 %collective-permute-done.27.refs_11_.refs_27_ = f32[4,2,64,256]{3,2,1,0:T(8,128)S(1)} collective-permute-done((f32[4,2,64,256]{3,2,1,0:T(8,128)S(1)}, f32[4,2,64,256]{3,2,1,0:T(8,128)S(1)}, u32[]{:S(2)}, u32[]{:S(2)}) %collective-permute-start.27) | collective-permute-done | bytes 524320 | tf_op jit(solution)/shard_map/ppermute | solution.py:30
  193.7 8.5 %product.3 = (f32[1024,256]{1,0:T(8,128)S(1)}, f32[1024,256]{1,0:T(8,128)S(1)}) custom-call(s32[6]{0:T(128)S(1)} %stack.76.s_ref, bf16[1024,1024]{1,0:T(8,128)(2,1)S(1)} %bitcast.43, bf16[1024,1024]{1,0:T(8,128)(2,1)S(1)} %bitcast.45, bf16[1024,1024]{1,0:T(8,128)(2,1)S(1)} %bitcast.47, bf16[1024,1024]{1,0:T(8,128)(2,1)S(1)} %bitcast.49, ...), custom_call_target="tpu_custom_call" | custom-call | flops 6442450944 | bytes 12582912 | tf_op jit(solution)/shard_map/product/pallas_call | solution.py:219
  202.3 9.9 %collective-permute-start.44 = (f32[1024,256]{1,0:T(8,128)S(1)}, f32[1024,256]{1,0:T(8,128)}, u32[]{:S(2)}, u32[]{:S(2)}) collective-permute-start(f32[1024,256]{1,0:T(8,128)S(1)} %get-tuple-element.36), channel_id=1, source_target_pairs={{0,96},{1,112},{2,66},{3,82},{4,36},{5,52},{6,6},{7,22},{8,224},{9... | collective-permute-start | bytes 3145736 | tf_op jit(solution)/shard_map/ppermute | solution.py:30
  212.2 2.3 collective-permute-start.37
  214.6 3.8 collective-permute-start.46
  218.4 9.3 %product.2 = (f32[1024,256]{1,0:T(8,128)S(1)}, f32[1024,256]{1,0:T(8,128)}) custom-call(s32[6]{0:T(128)S(1)} %stack.76.s_ref, bf16[1024,1024]{1,0:T(8,128)(2,1)S(1)} %bitcast.44, bf16[1024,1024]{1,0:T(8,128)(2,1)S(1)} %bitcast.46, bf16[1024,1024]{1,0:T(8,128)(2,1)S(1)} %bitcast.48, bf16[1024,1024]{1,0:T(8,128)(2,1)S(1)} %bitcast.50, ...), custom_call_target="tpu_custom_call" | custom-call | flops 6442450944 | bytes 12582912 | tf_op jit(solution)/shard_map/product/pallas_call | solution.py:219
  227.7 2.3 collective-permute-start.40
  230.0 7.4 %collective-permute-start.42 = (f32[1024,256]{1,0:T(8,128)}, f32[1024,256]{1,0:T(8,128)}, u32[]{:S(2)}, u32[]{:S(2)}) collective-permute-start(f32[1024,256]{1,0:T(8,128)} %get-tuple-element.37), channel_id=1, source_target_pairs={{0,64},{1,80},{2,34},{3,50},{4,4},{5,20},{6,102},{7,118},{8,192},{... | collective-permute-start | bytes 3145736 | tf_op jit(solution)/shard_map/ppermute | solution.py:30
  237.5 21.6 %collective-permute-done.44 = f32[1024,256]{1,0:T(8,128)} collective-permute-done((f32[1024,256]{1,0:T(8,128)S(1)}, f32[1024,256]{1,0:T(8,128)}, u32[]{:S(2)}, u32[]{:S(2)}) %collective-permute-start.44) | collective-permute-done | bytes 1048608 | tf_op jit(solution)/shard_map/ppermute | solution.py:30
  259.0 1.9 collective-permute-start.39
  261.0 2.1 collective-permute-start.36
  263.1 6.5 %collective-permute-done.46 = f32[1024,256]{1,0:T(8,128)} collective-permute-done((f32[1024,256]{1,0:T(8,128)S(1)}, f32[1024,256]{1,0:T(8,128)}, u32[]{:S(2)}, u32[]{:S(2)}) %collective-permute-start.46) | collective-permute-done | bytes 1048608 | tf_op jit(solution)/shard_map/ppermute | solution.py:30
  269.6 9.5 %collective-permute-start.38 = (f32[1024,256]{1,0:T(8,128)}, f32[1024,256]{1,0:T(8,128)}, u32[]{:S(2)}, u32[]{:S(2)}) collective-permute-start(f32[1024,256]{1,0:T(8,128)} %get-tuple-element.37), channel_id=1, source_target_pairs={{0,4},{1,5},{2,2},{3,3},{4,0},{5,1},{6,6},{7,7},{8,12},{9,13},{10,... | collective-permute-start | bytes 3145736 | tf_op jit(solution)/shard_map/ppermute | solution.py:30
  279.0 14.8 %collective-permute-done.40 = f32[1024,256]{1,0:T(8,128)} collective-permute-done((f32[1024,256]{1,0:T(8,128)S(1)}, f32[1024,256]{1,0:T(8,128)}, u32[]{:S(2)}, u32[]{:S(2)}) %collective-permute-start.40) | collective-permute-done | bytes 1048608 | tf_op jit(solution)/shard_map/ppermute | solution.py:30
  293.8 20.8 %collective-permute-start.41 = (f32[1024,256]{1,0:T(8,128)}, f32[1024,256]{1,0:T(8,128)}, u32[]{:S(2)}, u32[]{:S(2)}) collective-permute-start(f32[1024,256]{1,0:T(8,128)} %collective-permute-done.40), channel_id=1, source_target_pairs={{0,0},{1,1},{2,2},{3,3},{4,4},{5,5},{6,6},{7,7},{8,8},{9,9},{10,10... | collective-permute-start | bytes 3145736 | tf_op jit(solution)/shard_map/ppermute | solution.py:30
  314.7 9.4 %collective-permute-start.43 = (f32[1024,256]{1,0:T(8,128)}, f32[1024,256]{1,0:T(8,128)}, u32[]{:S(2)}, u32[]{:S(2)}) collective-permute-start(f32[1024,256]{1,0:T(8,128)} %collective-permute-done.42), channel_id=1, source_target_pairs={{0,4},{1,5},{2,6},{3,7},{4,0},{5,1},{6,2},{7,3},{8,12},{9,13},{10,... | collective-permute-start | bytes 3145736 | tf_op jit(solution)/shard_map/ppermute | solution.py:30
  324.1 1.9 collective-permute-start.45
  326.1 45.5 %collective-permute-start.47 = (f32[1024,256]{1,0:T(8,128)}, f32[1024,256]{1,0:T(8,128)}, u32[]{:S(2)}, u32[]{:S(2)}) collective-permute-start(f32[1024,256]{1,0:T(8,128)} %collective-permute-done.46), channel_id=1, source_target_pairs={{0,6},{1,7},{2,0},{3,1},{4,2},{5,3},{6,4},{7,5},{8,134},{9,135},{1... | collective-permute-start | bytes 3145736 | tf_op jit(solution)/shard_map/ppermute | solution.py:30
  371.7 4.5 %gather_fusion = f32[1024]{0:T(1024)S(1)} fusion(f32[1024]{0:T(1024)S(1)} %copy-done, s32[1024]{0:T(1024)S(1)} %fusion.1), kind=kCustom, calls=%fused_computation | custom fusion | bytes 12288 | tf_op jit(solution)/shard_map/jit(_take)/gather | solution.py:374
  378.6 2.2 copy-done.3
  382.0 4.9 %begin.1 = (f32[1024,1024]{1,0:T(8,128)}, f32[1024,1024]{1,0:T(8,128)S(1)}) custom-call(s32[6]{0:T(128)S(1)} %stack.76.s_ref, f32[1024,1024]{1,0:T(8,128)S(1)} %bitcast.42, f32[1,1]{1,0:T(1,128)} %bitcast.9.e_pair, f32[1,1024]{1,0:T(1,128)S(1)} %bitcast.52, f32[1024,1]{1,0:T(8,128)S(1)} %copy.13.e_col, f32[1024,256]{1,0:T(8,128)S(1)} %copy-done.5, ...), custom_call_target="tpu_custom_call" | custom-call | tf_op jit(solution)/shard_map/begin/pallas_call | solution.py:253
  387.0 4.4 %finish.4.total = f32[1024,1024]{1,0:T(8,128)} custom-call(s32[6]{0:T(128)S(1)} %stack.76.s_ref, f32[1024,1024]{1,0:T(8,128)} %get-tuple-element.39.total, f32[1024,1024]{1,0:T(8,128)S(1)} %get-tuple-element.40.inverse, f32[1024,256]{1,0:T(8,128)} %collective-permute-done.41.mirror), custom_call_target="tpu_custom_call", output_to_operand_aliasing={{}: (1, {})} | custom-call | tf_op jit(solution)/shard_map/finish/pallas_call | solution.py:282
  391.3 4.4 %finish.5.total = f32[1024,1024]{1,0:T(8,128)} custom-call(s32[6]{0:T(128)S(1)} %stack.76.s_ref, f32[1024,1024]{1,0:T(8,128)} %finish.4.total, f32[1024,1024]{1,0:T(8,128)S(1)} %get-tuple-element.40.inverse, f32[1024,256]{1,0:T(8,128)} %collective-permute-done.43.mirror), custom_call_target="tpu_custom_call", output_to_operand_aliasing={{}: (1, {})} | custom-call | tf_op jit(solution)/shard_map/finish/pallas_call | solution.py:282
  395.7 4.4 %finish.6.total = f32[1024,1024]{1,0:T(8,128)} custom-call(s32[6]{0:T(128)S(1)} %stack.76.s_ref, f32[1024,1024]{1,0:T(8,128)} %finish.5.total, f32[1024,1024]{1,0:T(8,128)S(1)} %get-tuple-element.40.inverse, f32[1024,256]{1,0:T(8,128)} %collective-permute-done.45.mirror), custom_call_target="tpu_custom_call", output_to_operand_aliasing={{}: (1, {})} | custom-call | tf_op jit(solution)/shard_map/finish/pallas_call | solution.py:282
  400.0 4.4 %finish.7 = f32[1024,1024]{1,0:T(8,128)} custom-call(s32[6]{0:T(128)S(1)} %stack.76.s_ref, f32[1024,1024]{1,0:T(8,128)} %finish.6.total, f32[1024,1024]{1,0:T(8,128)S(1)} %get-tuple-element.40.inverse, f32[1024,256]{1,0:T(8,128)} %collective-permute-done.47.mirror), custom_call_target="tpu_custom_call", output_to_operand_aliasing={{}: (1, {})} | custom-call | tf_op jit(solution)/shard_map/finish/pallas_call | solution.py:282
  (98 shorter events, 37.3 us)
Async XLA Ops:
  0.0 20.9 %collective-permute-start.9 = (f32[1024,1024]{1,0:T(8,128)}, f32[1024,1024]{1,0:T(8,128)}, u32[]{:S(2)}, u32[]{:S(2)}) collective-permute-start(f32[1024,1024]{1,0:T(8,128)} %bitcast.37), channel_id=1, source_target_pairs={{0,1},{1,0},{2,3},{3,2},{4,5},{5,4},{6,7},{7,6},{8,9},{9,8},{10,11... | collective-permute-start | bytes 12582920 | tf_op jit(solution)/shard_map/ppermute | solution.py:30
  10.7 5.0 %collective-permute-start = (f32[2,128,1024]{2,1,0:T(8,128)}, f32[2,128,1024]{2,1,0:T(8,128)}, u32[]{:S(2)}, u32[]{:S(2)}) collective-permute-start(f32[2,128,1024]{2,1,0:T(8,128)} %get-tuple-element.23), channel_id=1, source_target_pairs={{15,13},{31,29},{47,45},{63,61},{79,77},{95,93},{111,109},{127,125... | collective-permute-start | bytes 3145736 | tf_op jit(solution)/shard_map/ppermute | solution.py:30
  12.4 3.3 collective-permute-start.1
  14.0 1.7 collective-permute-start.2
  18.2 11.4 %collective-permute-start.3 = (f32[128,1024]{1,0:T(8,128)}, f32[128,1024]{1,0:T(8,128)}, u32[]{:S(2)}, u32[]{:S(2)}) collective-permute-start(f32[128,1024]{1,0:T(8,128)} %slice_bitcast_fusion), channel_id=1, source_target_pairs={{1,0},{3,2},{5,4},{7,6},{9,8},{11,10},{13,12},{15,14},{17,16},{19,... | collective-permute-start | bytes 1572872 | tf_op jit(solution)/shard_map/ppermute | solution.py:30
  27.3 14.1 %collective-permute-start.10 = (f32[128,1024]{1,0:T(8,128)S(1)}, f32[128,1024]{1,0:T(8,128)}, u32[]{:S(2)}, u32[]{:S(2)}) collective-permute-start(f32[128,1024]{1,0:T(8,128)S(1)} %get-tuple-element.29), channel_id=1, source_target_pairs={{0,6},{1,7},{2,0},{3,1},{4,2},{5,3},{6,4},{7,5},{8,14},{9,15},{10,... | collective-permute-start | bytes 1572872 | tf_op jit(solution)/shard_map/ppermute | solution.py:30
  27.6 24.2 %collective-permute-start.11 = (f32[128,1024]{1,0:T(8,128)S(1)}, f32[128,1024]{1,0:T(8,128)}, u32[]{:S(2)}, u32[]{:S(2)}) collective-permute-start(f32[128,1024]{1,0:T(8,128)S(1)} %get-tuple-element.30), channel_id=1, source_target_pairs={{0,4},{1,5},{2,6},{3,7},{4,0},{5,1},{6,2},{7,3},{8,12},{9,13},{10,... | collective-permute-start | bytes 1572872 | tf_op jit(solution)/shard_map/ppermute | solution.py:30
  29.0 25.3 %collective-permute-start.12 = (f32[128,1024]{1,0:T(8,128)S(1)}, f32[128,1024]{1,0:T(8,128)}, u32[]{:S(2)}, u32[]{:S(2)}) collective-permute-start(f32[128,1024]{1,0:T(8,128)S(1)} %get-tuple-element.31), channel_id=1, source_target_pairs={{0,2},{1,3},{2,4},{3,5},{4,6},{5,7},{6,0},{7,1},{8,10},{9,11},{10,... | collective-permute-start | bytes 1572872 | tf_op jit(solution)/shard_map/ppermute | solution.py:30
  30.4 58.8 %collective-permute-start.4 = (f32[128,1024]{1,0:T(8,128)}, f32[128,1024]{1,0:T(8,128)S(1)}, u32[]{:S(2)}, u32[]{:S(2)}) collective-permute-start(f32[128,1024]{1,0:T(8,128)} %fusion), channel_id=1, source_target_pairs={{8,0},{9,1},{10,2},{11,3},{12,4},{13,5},{14,6},{15,7},{24,16},{25,... | collective-permute-start | bytes 1572872 | tf_op jit(solution)/shard_map/ppermute | solution.py:30
  32.5 56.9 %collective-permute-start.20 = (f32[2,64,256]{2,1,0:T(8,128)}, f32[2,64,256]{2,1,0:T(8,128)S(1)}, u32[]{:S(2)}, u32[]{:S(2)}) collective-permute-start(f32[2,64,256]{2,1,0:T(8,128)} %get-tuple-element.42), channel_id=1, source_target_pairs={{0,6},{1,7},{2,0},{3,1},{4,2},{5,3},{6,4},{7,5},{8,14},{9,15},{10,... | collective-permute-start | bytes 393224 | tf_op jit(solution)/shard_map/ppermute | solution.py:30
  41.4 48.8 %collective-permute-start.19 = (f32[2,64,256]{2,1,0:T(8,128)S(1)}, f32[2,64,256]{2,1,0:T(8,128)S(1)}, u32[]{:S(2)}, u32[]{:S(2)}) collective-permute-start(f32[2,64,256]{2,1,0:T(8,128)S(1)} %get-tuple-element.43), channel_id=1, source_target_pairs={{0,4},{1,5},{2,6},{3,7},{4,0},{5,1},{6,2},{7,3},{8,12},{9,13},{10,... | collective-permute-start | bytes 393224 | tf_op jit(solution)/shard_map/ppermute | solution.py:30
  51.7 40.4 %collective-permute-start.18 = (f32[2,64,256]{2,1,0:T(8,128)S(1)}, f32[2,64,256]{2,1,0:T(8,128)S(1)}, u32[]{:S(2)}, u32[]{:S(2)}) collective-permute-start(f32[2,64,256]{2,1,0:T(8,128)S(1)} %get-tuple-element.44), channel_id=1, source_target_pairs={{0,2},{1,3},{2,4},{3,5},{4,6},{5,7},{6,0},{7,1},{8,10},{9,11},{10,... | collective-permute-start | bytes 393224 | tf_op jit(solution)/shard_map/ppermute | solution.py:30
  55.5 40.6 %collective-permute-start.13 = (f32[128,1024]{1,0:T(8,128)S(1)}, f32[128,1024]{1,0:T(8,128)}, u32[]{:S(2)}, u32[]{:S(2)}) collective-permute-start(f32[128,1024]{1,0:T(8,128)S(1)} %select_select_fusion.1), channel_id=1, source_target_pairs={{0,8},{1,9},{2,10},{3,11},{4,12},{5,13},{6,14},{7,15},{8,0},{9,1},... | collective-permute-start | bytes 1572872 | tf_op jit(solution)/shard_map/ppermute | solution.py:30
  89.3 8.4 %collective-permute-start.7 = (f32[128,1024]{1,0:T(8,128)S(1)}, f32[128,1024]{1,0:T(8,128)S(1)}, u32[]{:S(2)}, u32[]{:S(2)}) collective-permute-start(f32[128,1024]{1,0:T(8,128)S(1)} %broadcast_select_fusion.1), channel_id=1, source_target_pairs={{0,6},{1,7},{2,0},{3,1},{4,2},{5,3},{6,4},{7,5},{8,14},{9,15},{10,... | collective-permute-start | bytes 1572872 | tf_op jit(solution)/shard_map/ppermute | solution.py:30
  89.4 14.2 %collective-permute-start.6 = (f32[128,1024]{1,0:T(8,128)S(1)}, f32[128,1024]{1,0:T(8,128)}, u32[]{:S(2)}, u32[]{:S(2)}) collective-permute-start(f32[128,1024]{1,0:T(8,128)S(1)} %broadcast_select_fusion.1), channel_id=1, source_target_pairs={{0,4},{1,5},{2,6},{3,7},{4,0},{5,1},{6,2},{7,3},{8,12},{9,13},{10,... | collective-permute-start | bytes 1572872 | tf_op jit(solution)/shard_map/ppermute | solution.py:30
  90.2 15.6 %collective-permute-start.5 = (f32[128,1024]{1,0:T(8,128)S(1)}, f32[128,1024]{1,0:T(8,128)}, u32[]{:S(2)}, u32[]{:S(2)}) collective-permute-start(f32[128,1024]{1,0:T(8,128)S(1)} %broadcast_select_fusion.1), channel_id=1, source_target_pairs={{0,2},{1,3},{2,4},{3,5},{4,6},{5,7},{6,0},{7,1},{8,10},{9,11},{10,... | collective-permute-start | bytes 1572872 | tf_op jit(solution)/shard_map/ppermute | solution.py:30
  92.1 15.1 %collective-permute-start.28 = (f32[4,2,64,256]{3,2,1,0:T(8,128)S(1)}, f32[4,2,64,256]{3,2,1,0:T(8,128)S(1)}, u32[]{:S(2)}, u32[]{:S(2)}) collective-permute-start(f32[4,2,64,256]{3,2,1,0:T(8,128)S(1)} %pad_maximum_fusion.2.refs_4_.refs_20_), channel_id=1, source_target_pairs={{0,128},{1,129},{2,130},{3,131},{4,132},{5,133},{6,134},{7,135},{8... | collective-permute-start | bytes 1572872 | tf_op jit(solution)/shard_map/ppermute | solution.py:30
  97.2 11.5 %collective-permute-start.16 = (f32[128,1024]{1,0:T(8,128)S(1)}, f32[128,1024]{1,0:T(8,128)S(1)}, u32[]{:S(2)}, u32[]{:S(2)}) collective-permute-start(f32[128,1024]{1,0:T(8,128)S(1)} %broadcast_select_fusion), channel_id=1, source_target_pairs={{0,6},{1,7},{2,0},{3,1},{4,2},{5,3},{6,4},{7,5},{8,14},{9,15},{10,... | collective-permute-start | bytes 1572872 | tf_op jit(solution)/shard_map/ppermute | solution.py:30
  97.7 13.8 %collective-permute-start.15 = (f32[128,1024]{1,0:T(8,128)S(1)}, f32[128,1024]{1,0:T(8,128)S(1)}, u32[]{:S(2)}, u32[]{:S(2)}) collective-permute-start(f32[128,1024]{1,0:T(8,128)S(1)} %broadcast_select_fusion), channel_id=1, source_target_pairs={{0,4},{1,5},{2,6},{3,7},{4,0},{5,1},{6,2},{7,3},{8,12},{9,13},{10,... | collective-permute-start | bytes 1572872 | tf_op jit(solution)/shard_map/ppermute | solution.py:30
  103.6 13.7 %collective-permute-start.14 = (f32[128,1024]{1,0:T(8,128)S(1)}, f32[128,1024]{1,0:T(8,128)S(1)}, u32[]{:S(2)}, u32[]{:S(2)}) collective-permute-start(f32[128,1024]{1,0:T(8,128)S(1)} %broadcast_select_fusion), channel_id=1, source_target_pairs={{0,2},{1,3},{2,4},{3,5},{4,6},{5,7},{6,0},{7,1},{8,10},{9,11},{10,... | collective-permute-start | bytes 1572872 | tf_op jit(solution)/shard_map/ppermute | solution.py:30
  105.8 11.8 %collective-permute-start.22 = (f32[4,2,64,256]{3,2,1,0:T(8,128)S(1)}, f32[4,2,64,256]{3,2,1,0:T(8,128)S(1)}, u32[]{:S(2)}, u32[]{:S(2)}) collective-permute-start(f32[4,2,64,256]{3,2,1,0:T(8,128)S(1)} %pad_maximum_fusion.2.refs_4_.refs_20_), channel_id=1, source_target_pairs={{0,112},{1,113},{2,114},{3,115},{4,116},{5,117},{6,118},{7,119},{8... | collective-permute-start | bytes 1572872 | tf_op jit(solution)/shard_map/ppermute | solution.py:30
  107.2 61.5 %collective-permute-start.8 = (f32[4,128,1024]{2,1,0:T(8,128)S(1)}, f32[4,128,1024]{2,1,0:T(8,128)S(1)}, u32[]{:S(2)}, u32[]{:S(2)}) collective-permute-start(f32[4,128,1024]{2,1,0:T(8,128)S(1)} %pad_maximum_fusion.own), channel_id=1, source_target_pairs={{0,1},{1,0},{2,3},{3,2},{4,5},{5,4},{6,7},{7,6},{8,9},{9,8},{10,11... | collective-permute-start | bytes 6291464 | tf_op jit(solution)/shard_map/ppermute | solution.py:30
  108.7 15.1 %collective-permute-start.21 = (f32[4,2,64,256]{3,2,1,0:T(8,128)S(1)}, f32[4,2,64,256]{3,2,1,0:T(8,128)S(1)}, u32[]{:S(2)}, u32[]{:S(2)}) collective-permute-start(f32[4,2,64,256]{3,2,1,0:T(8,128)S(1)} %pad_maximum_fusion.2.refs_4_.refs_20_), channel_id=1, source_target_pairs={{0,16},{1,17},{2,18},{3,19},{4,20},{5,21},{6,22},{7,23},{8,24},{9,... | collective-permute-start | bytes 1572872 | tf_op jit(solution)/shard_map/ppermute | solution.py:30
  111.5 13.9 %collective-permute-start.30 = (f32[4,2,64,256]{3,2,1,0:T(8,128)S(1)}, f32[4,2,64,256]{3,2,1,0:T(8,128)S(1)}, u32[]{:S(2)}, u32[]{:S(2)}) collective-permute-start(f32[4,2,64,256]{3,2,1,0:T(8,128)S(1)} %collective-permute-done.28.refs_12_.refs_28_), channel_id=1, source_target_pairs={{0,112},{1,113},{2,114},{3,115},{4,116},{5,117},{6,118},{7,119},{8... | collective-permute-start | bytes 1572872 | tf_op jit(solution)/shard_map/ppermute | solution.py:30
  117.5 55.3 %collective-permute-start.17 = (f32[4,128,1024]{2,1,0:T(8,128)S(1)}, f32[4,128,1024]{2,1,0:T(8,128)S(1)}, u32[]{:S(2)}, u32[]{:S(2)}) collective-permute-start(f32[4,128,1024]{2,1,0:T(8,128)S(1)} %pad_maximum_fusion.1.own), channel_id=1, source_target_pairs={{0,1},{1,0},{2,3},{3,2},{4,5},{5,4},{6,7},{7,6},{8,9},{9,8},{10,11... | collective-permute-start | bytes 6291464 | tf_op jit(solution)/shard_map/ppermute | solution.py:30
  117.6 17.5 %collective-permute-start.29 = (f32[4,2,64,256]{3,2,1,0:T(8,128)S(1)}, f32[4,2,64,256]{3,2,1,0:T(8,128)S(1)}, u32[]{:S(2)}, u32[]{:S(2)}) collective-permute-start(f32[4,2,64,256]{3,2,1,0:T(8,128)S(1)} %collective-permute-done.28.refs_12_.refs_28_), channel_id=1, source_target_pairs={{0,16},{1,17},{2,18},{3,19},{4,20},{5,21},{6,22},{7,23},{8,24},{9,... | collective-permute-start | bytes 1572872 | tf_op jit(solution)/shard_map/ppermute | solution.py:30
  123.8 13.8 %collective-permute-start.24 = (f32[4,2,64,256]{3,2,1,0:T(8,128)S(1)}, f32[4,2,64,256]{3,2,1,0:T(8,128)S(1)}, u32[]{:S(2)}, u32[]{:S(2)}) collective-permute-start(f32[4,2,64,256]{3,2,1,0:T(8,128)S(1)} %collective-permute-done.22.refs_6_.refs_22_), channel_id=1, source_target_pairs={{0,112},{1,113},{2,114},{3,115},{4,116},{5,117},{6,118},{7,119},{8... | collective-permute-start | bytes 1572872 | tf_op jit(solution)/shard_map/ppermute | solution.py:30
  125.4 20.9 %collective-permute-start.23 = (f32[4,2,64,256]{3,2,1,0:T(8,128)S(1)}, f32[4,2,64,256]{3,2,1,0:T(8,128)S(1)}, u32[]{:S(2)}, u32[]{:S(2)}) collective-permute-start(f32[4,2,64,256]{3,2,1,0:T(8,128)S(1)} %collective-permute-done.21.refs_5_.refs_21_), channel_id=1, source_target_pairs={{0,16},{1,17},{2,18},{3,19},{4,20},{5,21},{6,22},{7,23},{8,24},{9,... | collective-permute-start | bytes 1572872 | tf_op jit(solution)/shard_map/ppermute | solution.py:30
  135.1 13.8 %collective-permute-start.32 = (f32[4,2,64,256]{3,2,1,0:T(8,128)S(1)}, f32[4,2,64,256]{3,2,1,0:T(8,128)S(1)}, u32[]{:S(2)}, u32[]{:S(2)}) collective-permute-start(f32[4,2,64,256]{3,2,1,0:T(8,128)S(1)} %collective-permute-done.30.refs_14_.refs_30_), channel_id=1, source_target_pairs={{0,112},{1,113},{2,114},{3,115},{4,116},{5,117},{6,118},{7,119},{8... | collective-permute-start | bytes 1572872 | tf_op jit(solution)/shard_map/ppermute | solution.py:30
  137.7 19.9 %collective-permute-start.31 = (f32[4,2,64,256]{3,2,1,0:T(8,128)S(1)}, f32[4,2,64,256]{3,2,1,0:T(8,128)S(1)}, u32[]{:S(2)}, u32[]{:S(2)}) collective-permute-start(f32[4,2,64,256]{3,2,1,0:T(8,128)S(1)} %collective-permute-done.29.refs_13_.refs_29_), channel_id=1, source_target_pairs={{0,16},{1,17},{2,18},{3,19},{4,20},{5,21},{6,22},{7,23},{8,24},{9,... | collective-permute-start | bytes 1572872 | tf_op jit(solution)/shard_map/ppermute | solution.py:30
  146.3 21.8 %collective-permute-start.25 = (f32[4,2,64,256]{3,2,1,0:T(8,128)S(1)}, f32[4,2,64,256]{3,2,1,0:T(8,128)S(1)}, u32[]{:S(2)}, u32[]{:S(2)}) collective-permute-start(f32[4,2,64,256]{3,2,1,0:T(8,128)S(1)} %collective-permute-done.23.refs_7_.refs_23_), channel_id=1, source_target_pairs={{0,16},{1,17},{2,18},{3,19},{4,20},{5,21},{6,22},{7,23},{8,24},{9,... | collective-permute-start | bytes 1572872 | tf_op jit(solution)/shard_map/ppermute | solution.py:30
  148.9 19.2 %collective-permute-start.34 = (f32[4,2,64,256]{3,2,1,0:T(8,128)S(1)}, f32[4,2,64,256]{3,2,1,0:T(8,128)S(1)}, u32[]{:S(2)}, u32[]{:S(2)}) collective-permute-start(f32[4,2,64,256]{3,2,1,0:T(8,128)S(1)} %collective-permute-done.32.refs_16_.refs_32_), channel_id=1, source_target_pairs={{0,112},{1,113},{2,114},{3,115},{4,116},{5,117},{6,118},{7,119},{8... | collective-permute-start | bytes 1572872 | tf_op jit(solution)/shard_map/ppermute | solution.py:30
  157.5 17.1 %collective-permute-start.26 = (f32[4,2,64,256]{3,2,1,0:T(8,128)S(1)}, f32[4,2,64,256]{3,2,1,0:T(8,128)S(1)}, u32[]{:S(2)}, u32[]{:S(2)}) collective-permute-start(f32[4,2,64,256]{3,2,1,0:T(8,128)S(1)} %collective-permute-done.24.refs_8_.refs_24_), channel_id=1, source_target_pairs={{0,112},{1,113},{2,114},{3,115},{4,116},{5,117},{6,118},{7,119},{8... | collective-permute-start | bytes 1572872 | tf_op jit(solution)/shard_map/ppermute | solution.py:30
  168.1 14.4 %collective-permute-start.33 = (f32[4,2,64,256]{3,2,1,0:T(8,128)S(1)}, f32[4,2,64,256]{3,2,1,0:T(8,128)S(1)}, u32[]{:S(2)}, u32[]{:S(2)}) collective-permute-start(f32[4,2,64,256]{3,2,1,0:T(8,128)S(1)} %collective-permute-done.31.refs_15_.refs_31_), channel_id=1, source_target_pairs={{0,16},{1,17},{2,18},{3,19},{4,20},{5,21},{6,22},{7,23},{8,24},{9,... | collective-permute-start | bytes 1572872 | tf_op jit(solution)/shard_map/ppermute | solution.py:30
  168.1 25.6 %collective-permute-start.27 = (f32[4,2,64,256]{3,2,1,0:T(8,128)S(1)}, f32[4,2,64,256]{3,2,1,0:T(8,128)S(1)}, u32[]{:S(2)}, u32[]{:S(2)}) collective-permute-start(f32[4,2,64,256]{3,2,1,0:T(8,128)S(1)} %collective-permute-done.25.refs_9_.refs_25_), channel_id=1, source_target_pairs={{0,16},{1,17},{2,18},{3,19},{4,20},{5,21},{6,22},{7,23},{8,24},{9,... | collective-permute-start | bytes 1572872 | tf_op jit(solution)/shard_map/ppermute | solution.py:30
  168.7 25.0 %collective-permute-start.35 = (f32[4,2,64,256]{3,2,1,0:T(8,128)S(1)}, f32[4,2,64,256]{3,2,1,0:T(8,128)S(1)}, u32[]{:S(2)}, u32[]{:S(2)}) collective-permute-start(f32[4,2,64,256]{3,2,1,0:T(8,128)S(1)} %collective-permute-done.34.refs_18_.refs_34_), channel_id=1, source_target_pairs={{0,112},{1,113},{2,114},{3,115},{4,116},{5,117},{6,118},{7,119},{8... | collective-permute-start | bytes 1572872 | tf_op jit(solution)/shard_map/ppermute | solution.py:30
  202.3 56.8 %collective-permute-start.44 = (f32[1024,256]{1,0:T(8,128)S(1)}, f32[1024,256]{1,0:T(8,128)}, u32[]{:S(2)}, u32[]{:S(2)}) collective-permute-start(f32[1024,256]{1,0:T(8,128)S(1)} %get-tuple-element.36), channel_id=1, source_target_pairs={{0,96},{1,112},{2,66},{3,82},{4,36},{5,52},{6,6},{7,22},{8,224},{9... | collective-permute-start | bytes 3145736 | tf_op jit(solution)/shard_map/ppermute | solution.py:30
  212.2 48.7 %collective-permute-start.37 = (f32[1024,256]{1,0:T(8,128)S(1)}, f32[1024,256]{1,0:T(8,128)S(1)}, u32[]{:S(2)}, u32[]{:S(2)}) collective-permute-start(f32[1024,256]{1,0:T(8,128)S(1)} %get-tuple-element.36), channel_id=1, source_target_pairs={{0,6},{1,7},{2,4},{3,5},{4,2},{5,3},{6,0},{7,1},{8,14},{9,15},{10,... | collective-permute-start | bytes 3145736 | tf_op jit(solution)/shard_map/ppermute | solution.py:30
  214.6 55.0 %collective-permute-start.46 = (f32[1024,256]{1,0:T(8,128)S(1)}, f32[1024,256]{1,0:T(8,128)}, u32[]{:S(2)}, u32[]{:S(2)}) collective-permute-start(f32[1024,256]{1,0:T(8,128)S(1)} %get-tuple-element.38), channel_id=1, source_target_pairs={{0,32},{1,48},{2,2},{3,18},{4,100},{5,116},{6,70},{7,86},{8,40},{9... | collective-permute-start | bytes 3145736 | tf_op jit(solution)/shard_map/ppermute | solution.py:30
  227.7 66.1 %collective-permute-start.40 = (f32[1024,256]{1,0:T(8,128)S(1)}, f32[1024,256]{1,0:T(8,128)}, u32[]{:S(2)}, u32[]{:S(2)}) collective-permute-start(f32[1024,256]{1,0:T(8,128)S(1)} %get-tuple-element.35), channel_id=1, source_target_pairs={{0,0},{1,16},{2,98},{3,114},{4,68},{5,84},{6,38},{7,54},{8,128},{9... | collective-permute-start | bytes 3145736 | tf_op jit(solution)/shard_map/ppermute | solution.py:30
  230.0 84.7 %collective-permute-start.42 = (f32[1024,256]{1,0:T(8,128)}, f32[1024,256]{1,0:T(8,128)}, u32[]{:S(2)}, u32[]{:S(2)}) collective-permute-start(f32[1024,256]{1,0:T(8,128)} %get-tuple-element.37), channel_id=1, source_target_pairs={{0,64},{1,80},{2,34},{3,50},{4,4},{5,20},{6,102},{7,118},{8,192},{... | collective-permute-start | bytes 3145736 | tf_op jit(solution)/shard_map/ppermute | solution.py:30
  259.0 65.1 %collective-permute-start.39 = (f32[1024,256]{1,0:T(8,128)S(1)}, f32[1024,256]{1,0:T(8,128)S(1)}, u32[]{:S(2)}, u32[]{:S(2)}) collective-permute-start(f32[1024,256]{1,0:T(8,128)S(1)} %get-tuple-element.38), channel_id=1, source_target_pairs={{0,2},{1,3},{2,0},{3,1},{4,6},{5,7},{6,4},{7,5},{8,10},{9,11},{10,... | collective-permute-start | bytes 3145736 | tf_op jit(solution)/shard_map/ppermute | solution.py:30
  261.0 65.1 %collective-permute-start.36 = (f32[1024,256]{1,0:T(8,128)S(1)}, f32[1024,256]{1,0:T(8,128)S(1)}, u32[]{:S(2)}, u32[]{:S(2)}) collective-permute-start(f32[1024,256]{1,0:T(8,128)S(1)} %get-tuple-element.35), channel_id=1, source_target_pairs={{0,0},{1,1},{2,6},{3,7},{4,4},{5,5},{6,2},{7,3},{8,8},{9,9},{10,14... | collective-permute-start | bytes 3145736 | tf_op jit(solution)/shard_map/ppermute | solution.py:30
  269.6 109.0 %collective-permute-start.38 = (f32[1024,256]{1,0:T(8,128)}, f32[1024,256]{1,0:T(8,128)}, u32[]{:S(2)}, u32[]{:S(2)}) collective-permute-start(f32[1024,256]{1,0:T(8,128)} %get-tuple-element.37), channel_id=1, source_target_pairs={{0,4},{1,5},{2,2},{3,3},{4,0},{5,1},{6,6},{7,7},{8,12},{9,13},{10,... | collective-permute-start | bytes 3145736 | tf_op jit(solution)/shard_map/ppermute | solution.py:30
  293.8 93.1 %collective-permute-start.41 = (f32[1024,256]{1,0:T(8,128)}, f32[1024,256]{1,0:T(8,128)}, u32[]{:S(2)}, u32[]{:S(2)}) collective-permute-start(f32[1024,256]{1,0:T(8,128)} %collective-permute-done.40), channel_id=1, source_target_pairs={{0,0},{1,1},{2,2},{3,3},{4,4},{5,5},{6,6},{7,7},{8,8},{9,9},{10,10... | collective-permute-start | bytes 3145736 | tf_op jit(solution)/shard_map/ppermute | solution.py:30
  314.7 76.6 %collective-permute-start.43 = (f32[1024,256]{1,0:T(8,128)}, f32[1024,256]{1,0:T(8,128)}, u32[]{:S(2)}, u32[]{:S(2)}) collective-permute-start(f32[1024,256]{1,0:T(8,128)} %collective-permute-done.42), channel_id=1, source_target_pairs={{0,4},{1,5},{2,6},{3,7},{4,0},{5,1},{6,2},{7,3},{8,12},{9,13},{10,... | collective-permute-start | bytes 3145736 | tf_op jit(solution)/shard_map/ppermute | solution.py:30
  324.1 71.5 %collective-permute-start.45 = (f32[1024,256]{1,0:T(8,128)}, f32[1024,256]{1,0:T(8,128)}, u32[]{:S(2)}, u32[]{:S(2)}) collective-permute-start(f32[1024,256]{1,0:T(8,128)} %collective-permute-done.44), channel_id=1, source_target_pairs={{0,2},{1,3},{2,4},{3,5},{4,6},{5,7},{6,0},{7,1},{8,10},{9,11},{10,... | collective-permute-start | bytes 3145736 | tf_op jit(solution)/shard_map/ppermute | solution.py:30
  326.1 74.0 %collective-permute-start.47 = (f32[1024,256]{1,0:T(8,128)}, f32[1024,256]{1,0:T(8,128)}, u32[]{:S(2)}, u32[]{:S(2)}) collective-permute-start(f32[1024,256]{1,0:T(8,128)} %collective-permute-done.46), channel_id=1, source_target_pairs={{0,6},{1,7},{2,0},{3,1},{4,2},{5,3},{6,4},{7,5},{8,134},{9,135},{1... | collective-permute-start | bytes 3145736 | tf_op jit(solution)/shard_map/ppermute | solution.py:30
  (10 other events, 604.9 us)
where the time goes:
time: 407 us; the launch traced here: 404 us
  starting transfers between devices  193 us (47%)
  waiting for transfers between devices  133 us (33%)
  Pallas kernels  52.2 us (13%)
  local copies, waits for them, and re-layouts  16.1 us (4%)
  other arithmetic  6.73 us (2%)
    ppermute x48, starting transfers between devices, permute(): return lax.ppermute(array, AXES, pairs)  193 us
    ppermute x48, waiting for transfers between devices, permute(): return lax.ppermute(array, AXES, pairs)  133 us
    pallas_call x2, Pallas kernels, product(): pl.pallas_call(functools.partial(product_kernel, where, len(ns)), grid_sp...  17.9 us
    pallas_call x4, Pallas kernels, finish(): pl.pallas_call(finish_kernel, grid_spec=pltpu.PrefetchScalarGridSpec(num_...  17.4 us
  transfers between devices with their start and end apart: 48, of which 21 were waited for; matrix products, arithmetic and copies ran while one was open for 4% of the time, Pallas kernels for 10%

commit v1 on v0

--- a/solution.py
+++ b/solution.py
@@ -248,7 +248,7 @@
 
 def begin(tile, e_pair, e_virt, direct, scal):
     v, w = tile.shape[0], direct[0].shape[1]
-    steps = 4
+    steps = 8
     row = lambda width: pl.BlockSpec((v // steps, width), lambda g, s: (g, 0))
     return pl.pallas_call(
         begin_kernel,
@@ -276,7 +276,7 @@
 
 def finish(n, total, inverse, mirror, scal):
     v, w = mirror.shape
-    steps = 4
+    steps = 8
     at = lambda s: (s[3] + 2 * NY - s[1] // 2 - n) % NY
     block = pl.BlockSpec((w, v // steps), lambda g, s: (at(s), g))
     return pl.pallas_call(
@@ -292,6 +292,15 @@
         name="finish",
         compiler_params=pltpu.CompilerParams(vmem_limit_bytes=24 * 2**20),
     )(scal, total, inverse, mirror)
+
+
+def around(block):
+    half = block.shape[0] // 2
+    up = permute(block, shift_y(1))
+    down = permute(block, shift_y(-1))
+    far_up = permute(up[:half], shift_y(1))
+    far_down = permute(down[half:], shift_y(-1))
+    return [block, up, jnp.concatenate([far_up, far_down]), down]
 
 
 def pick(index, arrays):
@@ -348,13 +357,13 @@
     a_one = jnp.where(c == NC - 1, a_one[1], a_d)
     a_x = permute(a_one, swap_xl, lambda xh, z, xl, y, c: xl == NXL - 1)
     a_two = jnp.where(xl == NXL - 1, a_one, a_x)
-    a_all = jnp.stack([a_two] + [permute(a_two, shift_y(i)) for i in range(1, NY)])
+    a_all = jnp.stack(around(a_two))
     a_core = permute(a_all, swap_core)
     b_got = [permute(cut_b[i], shift_y(i)) for i in range(1, NY)]
     b_one = pick((y - b_at) % NY, [cut_b[0]] + b_got)
     b_x = permute(b_one, swap_xl)
     b_two = jnp.where(xl == b_xl, b_one, b_x)
-    b_y = [b_two] + [permute(b_two, shift_y(i)) for i in range(1, NY)]
+    b_y = around(b_two)
     b_all = jnp.stack(b_y)
     b_core = permute(b_all, swap_core)
     tiles = lay(a_all, a_core, scal)

time: 407 us -> 408 us (level)
  the two profiles are of different devices: /device:TPU:149 before, /device:TPU:11 now
where the time goes in v1:
time: 408 us; the launch traced here: 405 us
  waiting for transfers between devices  223 us (55%)
  starting transfers between devices  94.3 us (23%)
  Pallas kernels  63 us (15%)
  local copies, waits for them, and re-layouts  14.3 us (4%)
  other arithmetic  7.07 us (2%)
    ppermute x50, waiting for transfers between devices, permute(): return lax.ppermute(array, AXES, pairs)  223 us
    ppermute x50, starting transfers between devices, permute(): return lax.ppermute(array, AXES, pairs)  94.3 us
    pallas_call x4, Pallas kernels, finish(): pl.pallas_call(finish_kernel, grid_spec=pltpu.PrefetchScalarGridSpec(num_...  25.6 us
    pallas_call x2, Pallas kernels, product(): pl.pallas_call(functools.partial(product_kernel, where, len(ns)), grid_sp...  18.1 us
  transfers between devices with their start and end apart: 50, of which 19 were waited for; matrix products, arithmetic and copies ran while one was open for 4% of the time, Pallas kernels for 12%

profile of v1, /device:TPU:11, one launch (start us, length us, event | category | flops | bytes accessed | tf_op | source)
XLA Modules:
  0.0 405.0 jit_solution(2801957768668051939)
XLA Ops:
  4.0 2.2 copy-done.1
  6.2 4.7 %form_own.1 = (f32[2,128,1024]{2,1,0:T(8,128)S(1)}, f32[2,128,1024]{2,1,0:T(8,128)S(1)}, f32[2,128,1024]{2,1,0:T(8,128)}, f32[2,128,1024]{2,1,0:T(8,128)}) custom-call(s32[6]{0:T(128)S(1)} %stack.76.s_ref, f32[1024,1024]{1,0:T(8,128)S(1)} %bitcast.40, f32[1024,1024]{1,0:T(8,128)S(1)} %bitcast.41), custom_call_target="tpu_custom_call" | custom-call | tf_op jit(solution)/shard_map/form_own/pallas_call | solution.py:104
  14.6 35.4 %collective-permute-done.1 = f32[2,128,1024]{2,1,0:T(8,128)} collective-permute-done((f32[2,128,1024]{2,1,0:T(8,128)}, f32[2,128,1024]{2,1,0:T(8,128)}, u32[]{:S(2)}, u32[]{:S(2)}) %collective-permute-start.1) | collective-permute-done | bytes 1048608 | tf_op jit(solution)/shard_map/ppermute | solution.py:30
  50.0 1.8 select_select_fusion
  52.7 2.1 collective-permute-start.3
  54.8 4.3 %form.1 = (f32[128,1024]{1,0:T(8,128)S(1)}, f32[128,1024]{1,0:T(8,128)S(1)}, f32[128,1024]{1,0:T(8,128)S(1)}, f32[128,1024]{1,0:T(8,128)S(1)}) custom-call(s32[6]{0:T(128)S(1)} %stack.76.s_ref, f32[1024,1024]{1,0:T(8,128)S(1)} %bitcast.42, f32[1024,1024]{1,0:T(8,128)S(1)} %bitcast.43, f32[1024,1024]{1,0:T(8,128)} %collective-permute-done.10.rows_got.cols_got, ...), custom_call_target="tpu_custom_call" | custom-call | tf_op jit(solution)/shard_map/form/pallas_call | solution.py:129
  62.9 10.0 %collective-permute-done.11 = f32[128,1024]{1,0:T(8,128)} collective-permute-done((f32[128,1024]{1,0:T(8,128)S(1)}, f32[128,1024]{1,0:T(8,128)}, u32[]{:S(2)}, u32[]{:S(2)}) %collective-permute-start.11) | collective-permute-done | bytes 524320 | tf_op jit(solution)/shard_map/ppermute | solution.py:30
  72.9 3.6 collective-permute-done.13
  81.9 4.3 %collective-permute-done.14 = f32[128,1024]{1,0:T(8,128)S(1)} collective-permute-done((f32[128,1024]{1,0:T(8,128)S(1)}, f32[128,1024]{1,0:T(8,128)S(1)}, u32[]{:S(2)}, u32[]{:S(2)}) %collective-permute-start.14) | collective-permute-done | bytes 524320 | tf_op jit(solution)/shard_map/ppermute | solution.py:30
  88.9 5.6 %collective-permute-done.7 = f32[128,1024]{1,0:T(8,128)S(1)} collective-permute-done((f32[128,1024]{1,0:T(8,128)S(1)}, f32[128,1024]{1,0:T(8,128)S(1)}, u32[]{:S(2)}, u32[]{:S(2)}) %collective-permute-start.7) | collective-permute-done | bytes 524320 | tf_op jit(solution)/shard_map/ppermute | solution.py:30
  95.6 10.2 %collective-permute-done.22 = f32[2,64,256]{2,1,0:T(8,128)S(1)} collective-permute-done((f32[2,64,256]{2,1,0:T(8,128)S(1)}, f32[2,64,256]{2,1,0:T(8,128)S(1)}, u32[]{:S(2)}, u32[]{:S(2)}) %collective-permute-start.22) | collective-permute-done | bytes 131104 | tf_op jit(solution)/shard_map/ppermute | solution.py:30
  105.9 6.9 %collective-permute-done.20 = f32[2,64,256]{2,1,0:T(8,128)S(1)} collective-permute-done((f32[2,64,256]{2,1,0:T(8,128)S(1)}, f32[2,64,256]{2,1,0:T(8,128)S(1)}, u32[]{:S(2)}, u32[]{:S(2)}) %collective-permute-start.20) | collective-permute-done | bytes 131104 | tf_op jit(solution)/shard_map/ppermute | solution.py:30
  112.8 1.9 collective-permute-start.30
  114.7 6.6 %collective-permute-start.24 = (f32[4,2,64,256]{3,2,1,0:T(8,128)S(1)}, f32[4,2,64,256]{3,2,1,0:T(8,128)S(1)}, u32[]{:S(2)}, u32[]{:S(2)}) collective-permute-start(f32[4,2,64,256]{3,2,1,0:T(8,128)S(1)} %pad_maximum_fusion.2.refs_4_.refs_20_), channel_id=1, source_target_pairs={{0,112},{1,113},{2,114},{3,115},{4,116},{5,117},{6,118},{7,119},{8... | collective-permute-start | bytes 1572872 | tf_op jit(solution)/shard_map/ppermute | solution.py:30
  123.4 1.9 collective-permute-start.23
  128.8 12.1 %collective-permute-done.23.refs_5_.refs_21_ = f32[4,2,64,256]{3,2,1,0:T(8,128)S(1)} collective-permute-done((f32[4,2,64,256]{3,2,1,0:T(8,128)S(1)}, f32[4,2,64,256]{3,2,1,0:T(8,128)S(1)}, u32[]{:S(2)}, u32[]{:S(2)}) %collective-permute-start.23) | collective-permute-done | bytes 524320 | tf_op jit(solution)/shard_map/ppermute | solution.py:30
  142.3 9.8 %collective-permute-done.31.refs_13_.refs_29_ = f32[4,2,64,256]{3,2,1,0:T(8,128)S(1)} collective-permute-done((f32[4,2,64,256]{3,2,1,0:T(8,128)S(1)}, f32[4,2,64,256]{3,2,1,0:T(8,128)S(1)}, u32[]{:S(2)}, u32[]{:S(2)}) %collective-permute-start.31) | collective-permute-done | bytes 524320 | tf_op jit(solution)/shard_map/ppermute | solution.py:30
  153.5 9.8 %collective-permute-done.25.refs_7_.refs_23_ = f32[4,2,64,256]{3,2,1,0:T(8,128)S(1)} collective-permute-done((f32[4,2,64,256]{3,2,1,0:T(8,128)S(1)}, f32[4,2,64,256]{3,2,1,0:T(8,128)S(1)}, u32[]{:S(2)}, u32[]{:S(2)}) %collective-permute-start.25) | collective-permute-done | bytes 524320 | tf_op jit(solution)/shard_map/ppermute | solution.py:30
  164.2 1.8 collective-permute-start.36
  166.0 8.6 %collective-permute-done.33.refs_15_.refs_31_ = f32[4,2,64,256]{3,2,1,0:T(8,128)S(1)} collective-permute-done((f32[4,2,64,256]{3,2,1,0:T(8,128)S(1)}, f32[4,2,64,256]{3,2,1,0:T(8,128)S(1)}, u32[]{:S(2)}, u32[]{:S(2)}) %collective-permute-start.33) | collective-permute-done | bytes 524320 | tf_op jit(solution)/shard_map/ppermute | solution.py:30
  176.0 8.1 %collective-permute-done.27.refs_9_.refs_25_ = f32[4,2,64,256]{3,2,1,0:T(8,128)S(1)} collective-permute-done((f32[4,2,64,256]{3,2,1,0:T(8,128)S(1)}, f32[4,2,64,256]{3,2,1,0:T(8,128)S(1)}, u32[]{:S(2)}, u32[]{:S(2)}) %collective-permute-start.27) | collective-permute-done | bytes 524320 | tf_op jit(solution)/shard_map/ppermute | solution.py:30
  184.1 2.7 collective-permute-start.37
  190.4 8.9 %collective-permute-done.35.refs_17_.refs_33_ = f32[4,2,64,256]{3,2,1,0:T(8,128)S(1)} collective-permute-done((f32[4,2,64,256]{3,2,1,0:T(8,128)S(1)}, f32[4,2,64,256]{3,2,1,0:T(8,128)S(1)}, u32[]{:S(2)}, u32[]{:S(2)}) %collective-permute-start.35) | collective-permute-done | bytes 524320 | tf_op jit(solution)/shard_map/ppermute | solution.py:30
  199.3 10.8 %collective-permute-done.29.refs_11_.refs_27_ = f32[4,2,64,256]{3,2,1,0:T(8,128)S(1)} collective-permute-done((f32[4,2,64,256]{3,2,1,0:T(8,128)S(1)}, f32[4,2,64,256]{3,2,1,0:T(8,128)S(1)}, u32[]{:S(2)}, u32[]{:S(2)}) %collective-permute-start.29) | collective-permute-done | bytes 524320 | tf_op jit(solution)/shard_map/ppermute | solution.py:30
  210.1 8.6 %product.3 = (f32[1024,256]{1,0:T(8,128)S(1)}, f32[1024,256]{1,0:T(8,128)S(1)}) custom-call(s32[6]{0:T(128)S(1)} %stack.76.s_ref, bf16[1024,1024]{1,0:T(8,128)(2,1)S(1)} %bitcast.45, bf16[1024,1024]{1,0:T(8,128)(2,1)S(1)} %bitcast.47, bf16[1024,1024]{1,0:T(8,128)(2,1)S(1)} %bitcast.49, bf16[1024,1024]{1,0:T(8,128)(2,1)S(1)} %bitcast.51, ...), custom_call_target="tpu_custom_call" | custom-call | flops 6442450944 | bytes 12582912 | tf_op jit(solution)/shard_map/product/pallas_call | solution.py:219
  218.8 2.1 collective-permute-start.46
  220.9 2.0 collective-permute-start.39
  222.9 5.2 %collective-permute-start.48 = (f32[1024,256]{1,0:T(8,128)S(1)}, f32[1024,256]{1,0:T(8,128)}, u32[]{:S(2)}, u32[]{:S(2)}) collective-permute-start(f32[1024,256]{1,0:T(8,128)S(1)} %get-tuple-element.38), channel_id=1, source_target_pairs={{0,32},{1,48},{2,2},{3,18},{4,100},{5,116},{6,70},{7,86},{8,40},{9... | collective-permute-start | bytes 3145736 | tf_op jit(solution)/shard_map/ppermute | solution.py:30
  228.2 9.4 %product.2 = (f32[1024,256]{1,0:T(8,128)S(1)}, f32[1024,256]{1,0:T(8,128)}) custom-call(s32[6]{0:T(128)S(1)} %stack.76.s_ref, bf16[1024,1024]{1,0:T(8,128)(2,1)S(1)} %bitcast.46, bf16[1024,1024]{1,0:T(8,128)(2,1)S(1)} %bitcast.48, bf16[1024,1024]{1,0:T(8,128)(2,1)S(1)} %bitcast.50, bf16[1024,1024]{1,0:T(8,128)(2,1)S(1)} %bitcast.52, ...), custom_call_target="tpu_custom_call" | custom-call | flops 6442450944 | bytes 12582912 | tf_op jit(solution)/shard_map/product/pallas_call | solution.py:219
  237.6 1.9 collective-permute-start.42
  239.5 6.3 %collective-permute-start.44 = (f32[1024,256]{1,0:T(8,128)}, f32[1024,256]{1,0:T(8,128)}, u32[]{:S(2)}, u32[]{:S(2)}) collective-permute-start(f32[1024,256]{1,0:T(8,128)} %get-tuple-element.37), channel_id=1, source_target_pairs={{0,64},{1,80},{2,34},{3,50},{4,4},{5,20},{6,102},{7,118},{8,192},{... | collective-permute-start | bytes 3145736 | tf_op jit(solution)/shard_map/ppermute | solution.py:30
  245.9 48.8 %collective-permute-done.46 = f32[1024,256]{1,0:T(8,128)} collective-permute-done((f32[1024,256]{1,0:T(8,128)S(1)}, f32[1024,256]{1,0:T(8,128)}, u32[]{:S(2)}, u32[]{:S(2)}) %collective-permute-start.46) | collective-permute-done | bytes 1048608 | tf_op jit(solution)/shard_map/ppermute | solution.py:30
  294.7 1.9 collective-permute-start.41
  296.6 1.9 collective-permute-start.38
  298.6 9.5 %collective-permute-start.40 = (f32[1024,256]{1,0:T(8,128)}, f32[1024,256]{1,0:T(8,128)}, u32[]{:S(2)}, u32[]{:S(2)}) collective-permute-start(f32[1024,256]{1,0:T(8,128)} %get-tuple-element.37), channel_id=1, source_target_pairs={{0,4},{1,5},{2,2},{3,3},{4,0},{5,1},{6,6},{7,7},{8,12},{9,13},{10,... | collective-permute-start | bytes 3145736 | tf_op jit(solution)/shard_map/ppermute | solution.py:30
  308.0 6.9 %collective-permute-done.42 = f32[1024,256]{1,0:T(8,128)} collective-permute-done((f32[1024,256]{1,0:T(8,128)S(1)}, f32[1024,256]{1,0:T(8,128)}, u32[]{:S(2)}, u32[]{:S(2)}) %collective-permute-start.42) | collective-permute-done | bytes 1048608 | tf_op jit(solution)/shard_map/ppermute | solution.py:30
  314.9 9.4 %collective-permute-start.43 = (f32[1024,256]{1,0:T(8,128)}, f32[1024,256]{1,0:T(8,128)}, u32[]{:S(2)}, u32[]{:S(2)}) collective-permute-start(f32[1024,256]{1,0:T(8,128)} %collective-permute-done.42), channel_id=1, source_target_pairs={{0,0},{1,1},{2,2},{3,3},{4,4},{5,5},{6,6},{7,7},{8,8},{9,9},{10,10... | collective-permute-start | bytes 3145736 | tf_op jit(solution)/shard_map/ppermute | solution.py:30
  324.4 12.5 %collective-permute-start.45 = (f32[1024,256]{1,0:T(8,128)}, f32[1024,256]{1,0:T(8,128)}, u32[]{:S(2)}, u32[]{:S(2)}) collective-permute-start(f32[1024,256]{1,0:T(8,128)} %collective-permute-done.44), channel_id=1, source_target_pairs={{0,4},{1,5},{2,6},{3,7},{4,0},{5,1},{6,2},{7,3},{8,12},{9,13},{10,... | collective-permute-start | bytes 3145736 | tf_op jit(solution)/shard_map/ppermute | solution.py:30
  336.9 1.9 collective-permute-start.47
  339.8 1.9 collective-permute-start.49
  341.8 4.5 %gather_fusion = f32[1024]{0:T(1024)S(1)} fusion(f32[1024]{0:T(1024)S(1)} %copy-done, s32[1024]{0:T(1024)S(1)} %fusion.1), kind=kCustom, calls=%fused_computation | custom fusion | bytes 12288 | tf_op jit(solution)/shard_map/jit(_take)/gather | solution.py:383
  348.5 2.2 copy-done.3
  351.9 6.8 %begin.1 = (f32[1024,1024]{1,0:T(8,128)}, f32[1024,1024]{1,0:T(8,128)S(1)}) custom-call(s32[6]{0:T(128)S(1)} %stack.76.s_ref, f32[1024,1024]{1,0:T(8,128)S(1)} %bitcast.44, f32[1,1]{1,0:T(1,128)} %bitcast.9.e_pair, f32[1,1024]{1,0:T(1,128)S(1)} %bitcast.54, f32[1024,1]{1,0:T(8,128)S(1)} %copy.13.e_col, f32[1024,256]{1,0:T(8,128)S(1)} %copy-done.5, ...), custom_call_target="tpu_custom_call" | custom-call | tf_op jit(solution)/shard_map/begin/pallas_call | solution.py:253
  358.8 6.4 %finish.4.total = f32[1024,1024]{1,0:T(8,128)} custom-call(s32[6]{0:T(128)S(1)} %stack.76.s_ref, f32[1024,1024]{1,0:T(8,128)} %get-tuple-element.39.total, f32[1024,1024]{1,0:T(8,128)S(1)} %get-tuple-element.40.inverse, f32[1024,256]{1,0:T(8,128)} %collective-permute-done.43.mirror), custom_call_target="tpu_custom_call", output_to_operand_aliasing={{}: (1, {})} | custom-call | tf_op jit(solution)/shard_map/finish/pallas_call | solution.py:282
  365.2 20.6 %collective-permute-done.45.mirror = f32[1024,256]{1,0:T(8,128)} collective-permute-done((f32[1024,256]{1,0:T(8,128)}, f32[1024,256]{1,0:T(8,128)}, u32[]{:S(2)}, u32[]{:S(2)}) %collective-permute-start.45) | collective-permute-done | bytes 1048608 | tf_op jit(solution)/shard_map/ppermute | solution.py:30
  385.8 6.4 %finish.5.total = f32[1024,1024]{1,0:T(8,128)} custom-call(s32[6]{0:T(128)S(1)} %stack.76.s_ref, f32[1024,1024]{1,0:T(8,128)} %finish.4.total, f32[1024,1024]{1,0:T(8,128)S(1)} %get-tuple-element.40.inverse, f32[1024,256]{1,0:T(8,128)} %collective-permute-done.45.mirror), custom_call_target="tpu_custom_call", output_to_operand_aliasing={{}: (1, {})} | custom-call | tf_op jit(solution)/shard_map/finish/pallas_call | solution.py:282
  392.2 6.4 %finish.6.total = f32[1024,1024]{1,0:T(8,128)} custom-call(s32[6]{0:T(128)S(1)} %stack.76.s_ref, f32[1024,1024]{1,0:T(8,128)} %finish.5.total, f32[1024,1024]{1,0:T(8,128)S(1)} %get-tuple-element.40.inverse, f32[1024,256]{1,0:T(8,128)} %collective-permute-done.47.mirror), custom_call_target="tpu_custom_call", output_to_operand_aliasing={{}: (1, {})} | custom-call | tf_op jit(solution)/shard_map/finish/pallas_call | solution.py:282
  398.6 6.4 %finish.7 = f32[1024,1024]{1,0:T(8,128)} custom-call(s32[6]{0:T(128)S(1)} %stack.76.s_ref, f32[1024,1024]{1,0:T(8,128)} %finish.6.total, f32[1024,1024]{1,0:T(8,128)S(1)} %get-tuple-element.40.inverse, f32[1024,256]{1,0:T(8,128)} %collective-permute-done.49.mirror), custom_call_target="tpu_custom_call", output_to_operand_aliasing={{}: (1, {})} | custom-call | tf_op jit(solution)/shard_map/finish/pallas_call | solution.py:282
  (108 shorter events, 36.9 us)
Async XLA Ops:
  0.0 54.8 %collective-permute-start.10 = (f32[1024,1024]{1,0:T(8,128)}, f32[1024,1024]{1,0:T(8,128)}, u32[]{:S(2)}, u32[]{:S(2)}) collective-permute-start(f32[1024,1024]{1,0:T(8,128)} %bitcast.39), channel_id=1, source_target_pairs={{0,1},{1,0},{2,3},{3,2},{4,5},{5,4},{6,7},{7,6},{8,9},{9,8},{10,11... | collective-permute-start | bytes 12582920 | tf_op jit(solution)/shard_map/ppermute | solution.py:30
  11.6 38.3 %collective-permute-start.1 = (f32[2,128,1024]{2,1,0:T(8,128)}, f32[2,128,1024]{2,1,0:T(8,128)}, u32[]{:S(2)}, u32[]{:S(2)}) collective-permute-start(f32[2,128,1024]{2,1,0:T(8,128)} %get-tuple-element.24), channel_id=1, source_target_pairs={{15,11},{31,27},{47,43},{63,59},{79,75},{95,91},{111,107},{127,123... | collective-permute-start | bytes 3145736 | tf_op jit(solution)/shard_map/ppermute | solution.py:30
  12.9 37.0 %collective-permute-start.2 = (f32[2,128,1024]{2,1,0:T(8,128)S(1)}, f32[2,128,1024]{2,1,0:T(8,128)}, u32[]{:S(2)}, u32[]{:S(2)}) collective-permute-start(f32[2,128,1024]{2,1,0:T(8,128)S(1)} %get-tuple-element.25), channel_id=1, source_target_pairs={{15,9},{31,25},{47,41},{63,57},{79,73},{95,89},{111,105},{127,121}... | collective-permute-start | bytes 3145736 | tf_op jit(solution)/shard_map/ppermute | solution.py:30
  52.7 7.9 %collective-permute-start.3 = (f32[128,1024]{1,0:T(8,128)}, f32[128,1024]{1,0:T(8,128)}, u32[]{:S(2)}, u32[]{:S(2)}) collective-permute-start(f32[128,1024]{1,0:T(8,128)} %slice_bitcast_fusion), channel_id=1, source_target_pairs={{1,0},{3,2},{5,4},{7,6},{9,8},{11,10},{13,12},{15,14},{17,16},{19,... | collective-permute-start | bytes 1572872 | tf_op jit(solution)/shard_map/ppermute | solution.py:30
  59.1 13.8 %collective-permute-start.11 = (f32[128,1024]{1,0:T(8,128)S(1)}, f32[128,1024]{1,0:T(8,128)}, u32[]{:S(2)}, u32[]{:S(2)}) collective-permute-start(f32[128,1024]{1,0:T(8,128)S(1)} %get-tuple-element.29), channel_id=1, source_target_pairs={{0,6},{1,7},{2,0},{3,1},{4,2},{5,3},{6,4},{7,5},{8,14},{9,15},{10,... | collective-permute-start | bytes 1572872 | tf_op jit(solution)/shard_map/ppermute | solution.py:30
  59.2 13.7 %collective-permute-start.12 = (f32[128,1024]{1,0:T(8,128)S(1)}, f32[128,1024]{1,0:T(8,128)}, u32[]{:S(2)}, u32[]{:S(2)}) collective-permute-start(f32[128,1024]{1,0:T(8,128)S(1)} %get-tuple-element.30), channel_id=1, source_target_pairs={{0,4},{1,5},{2,6},{3,7},{4,0},{5,1},{6,2},{7,3},{8,12},{9,13},{10,... | collective-permute-start | bytes 1572872 | tf_op jit(solution)/shard_map/ppermute | solution.py:30
  59.3 17.3 %collective-permute-start.13 = (f32[128,1024]{1,0:T(8,128)S(1)}, f32[128,1024]{1,0:T(8,128)}, u32[]{:S(2)}, u32[]{:S(2)}) collective-permute-start(f32[128,1024]{1,0:T(8,128)S(1)} %get-tuple-element.31), channel_id=1, source_target_pairs={{0,2},{1,3},{2,4},{3,5},{4,6},{5,7},{6,0},{7,1},{8,10},{9,11},{10,... | collective-permute-start | bytes 1572872 | tf_op jit(solution)/shard_map/ppermute | solution.py:30
  61.5 16.4 %collective-permute-start.4 = (f32[128,1024]{1,0:T(8,128)}, f32[128,1024]{1,0:T(8,128)S(1)}, u32[]{:S(2)}, u32[]{:S(2)}) collective-permute-start(f32[128,1024]{1,0:T(8,128)} %fusion), channel_id=1, source_target_pairs={{8,0},{9,1},{10,2},{11,3},{12,4},{13,5},{14,6},{15,7},{24,16},{25,... | collective-permute-start | bytes 1572872 | tf_op jit(solution)/shard_map/ppermute | solution.py:30
  77.8 8.4 %collective-permute-start.14 = (f32[128,1024]{1,0:T(8,128)S(1)}, f32[128,1024]{1,0:T(8,128)S(1)}, u32[]{:S(2)}, u32[]{:S(2)}) collective-permute-start(f32[128,1024]{1,0:T(8,128)S(1)} %select_select_fusion.1), channel_id=1, source_target_pairs={{0,8},{1,9},{2,10},{3,11},{4,12},{5,13},{6,14},{7,15},{8,0},{9,1},... | collective-permute-start | bytes 1572872 | tf_op jit(solution)/shard_map/ppermute | solution.py:30
  79.0 15.4 %collective-permute-start.7 = (f32[128,1024]{1,0:T(8,128)S(1)}, f32[128,1024]{1,0:T(8,128)S(1)}, u32[]{:S(2)}, u32[]{:S(2)}) collective-permute-start(f32[128,1024]{1,0:T(8,128)S(1)} %broadcast_select_fusion.1), channel_id=1, source_target_pairs={{0,6},{1,7},{2,0},{3,1},{4,2},{5,3},{6,4},{7,5},{8,14},{9,15},{10,... | collective-permute-start | bytes 1572872 | tf_op jit(solution)/shard_map/ppermute | solution.py:30
  80.1 15.3 %collective-permute-start.5 = (f32[128,1024]{1,0:T(8,128)S(1)}, f32[128,1024]{1,0:T(8,128)S(1)}, u32[]{:S(2)}, u32[]{:S(2)}) collective-permute-start(f32[128,1024]{1,0:T(8,128)S(1)} %broadcast_select_fusion.1), channel_id=1, source_target_pairs={{0,2},{1,3},{2,4},{3,5},{4,6},{5,7},{6,0},{7,1},{8,10},{9,11},{10,... | collective-permute-start | bytes 1572872 | tf_op jit(solution)/shard_map/ppermute | solution.py:30
  86.2 35.2 %collective-permute-start.17 = (f32[128,1024]{1,0:T(8,128)S(1)}, f32[128,1024]{1,0:T(8,128)S(1)}, u32[]{:S(2)}, u32[]{:S(2)}) collective-permute-start(f32[128,1024]{1,0:T(8,128)S(1)} %broadcast_select_fusion), channel_id=1, source_target_pairs={{0,6},{1,7},{2,0},{3,1},{4,2},{5,3},{6,4},{7,5},{8,14},{9,15},{10,... | collective-permute-start | bytes 1572872 | tf_op jit(solution)/shard_map/ppermute | solution.py:30
  87.3 34.2 %collective-permute-start.15 = (f32[128,1024]{1,0:T(8,128)S(1)}, f32[128,1024]{1,0:T(8,128)S(1)}, u32[]{:S(2)}, u32[]{:S(2)}) collective-permute-start(f32[128,1024]{1,0:T(8,128)S(1)} %broadcast_select_fusion), channel_id=1, source_target_pairs={{0,2},{1,3},{2,4},{3,5},{4,6},{5,7},{6,0},{7,1},{8,10},{9,11},{10,... | collective-permute-start | bytes 1572872 | tf_op jit(solution)/shard_map/ppermute | solution.py:30
  87.8 18.0 %collective-permute-start.22 = (f32[2,64,256]{2,1,0:T(8,128)S(1)}, f32[2,64,256]{2,1,0:T(8,128)S(1)}, u32[]{:S(2)}, u32[]{:S(2)}) collective-permute-start(f32[2,64,256]{2,1,0:T(8,128)S(1)} %get-tuple-element.42), channel_id=1, source_target_pairs={{0,6},{1,7},{2,0},{3,1},{4,2},{5,3},{6,4},{7,5},{8,14},{9,15},{10,... | collective-permute-start | bytes 393224 | tf_op jit(solution)/shard_map/ppermute | solution.py:30
  94.5 11.4 %collective-permute-start.21 = (f32[2,64,256]{2,1,0:T(8,128)S(1)}, f32[2,64,256]{2,1,0:T(8,128)S(1)}, u32[]{:S(2)}, u32[]{:S(2)}) collective-permute-start(f32[2,64,256]{2,1,0:T(8,128)S(1)} %get-tuple-element.43), channel_id=1, source_target_pairs={{0,4},{1,5},{2,6},{3,7},{4,0},{5,1},{6,2},{7,3},{8,12},{9,13},{10,... | collective-permute-start | bytes 393224 | tf_op jit(solution)/shard_map/ppermute | solution.py:30
  95.4 19.3 %collective-permute-start.8 = (f32[64,1024]{1,0:T(8,128)S(1)}, f32[64,1024]{1,0:T(8,128)S(1)}, u32[]{:S(2)}, u32[]{:S(2)}) collective-permute-start(f32[64,1024]{1,0:T(8,128)S(1)} %slice.38), channel_id=1, source_target_pairs={{0,6},{1,7},{2,0},{3,1},{4,2},{5,3},{6,4},{7,5},{8,14},{9,15},{10,... | collective-permute-start | bytes 786440 | tf_op jit(solution)/shard_map/ppermute | solution.py:30
  105.8 15.5 %collective-permute-start.6 = (f32[64,1024]{1,0:T(8,128)S(1)}, f32[64,1024]{1,0:T(8,128)S(1)}, u32[]{:S(2)}, u32[]{:S(2)}) collective-permute-start(f32[64,1024]{1,0:T(8,128)S(1)} %slice.37), channel_id=1, source_target_pairs={{0,2},{1,3},{2,4},{3,5},{4,6},{5,7},{6,0},{7,1},{8,10},{9,11},{10,... | collective-permute-start | bytes 786440 | tf_op jit(solution)/shard_map/ppermute | solution.py:30
  105.8 6.9 %collective-permute-start.20 = (f32[2,64,256]{2,1,0:T(8,128)S(1)}, f32[2,64,256]{2,1,0:T(8,128)S(1)}, u32[]{:S(2)}, u32[]{:S(2)}) collective-permute-start(f32[2,64,256]{2,1,0:T(8,128)S(1)} %get-tuple-element.44), channel_id=1, source_target_pairs={{0,2},{1,3},{2,4},{3,5},{4,6},{5,7},{6,0},{7,1},{8,10},{9,11},{10,... | collective-permute-start | bytes 393224 | tf_op jit(solution)/shard_map/ppermute | solution.py:30
  112.8 10.6 %collective-permute-start.30 = (f32[4,2,64,256]{3,2,1,0:T(8,128)S(1)}, f32[4,2,64,256]{3,2,1,0:T(8,128)S(1)}, u32[]{:S(2)}, u32[]{:S(2)}) collective-permute-start(f32[4,2,64,256]{3,2,1,0:T(8,128)S(1)} %pad_maximum_fusion.2.refs_4_.refs_20_), channel_id=1, source_target_pairs={{0,128},{1,129},{2,130},{3,131},{4,132},{5,133},{6,134},{7,135},{8... | collective-permute-start | bytes 1572872 | tf_op jit(solution)/shard_map/ppermute | solution.py:30
  114.7 13.9 %collective-permute-start.24 = (f32[4,2,64,256]{3,2,1,0:T(8,128)S(1)}, f32[4,2,64,256]{3,2,1,0:T(8,128)S(1)}, u32[]{:S(2)}, u32[]{:S(2)}) collective-permute-start(f32[4,2,64,256]{3,2,1,0:T(8,128)S(1)} %pad_maximum_fusion.2.refs_4_.refs_20_), channel_id=1, source_target_pairs={{0,112},{1,113},{2,114},{3,115},{4,116},{5,117},{6,118},{7,119},{8... | collective-permute-start | bytes 1572872 | tf_op jit(solution)/shard_map/ppermute | solution.py:30
  121.6 6.8 %collective-permute-start.16 = (f32[64,1024]{1,0:T(8,128)S(1)}, f32[64,1024]{1,0:T(8,128)S(1)}, u32[]{:S(2)}, u32[]{:S(2)}) collective-permute-start(f32[64,1024]{1,0:T(8,128)S(1)} %slice.39), channel_id=1, source_target_pairs={{0,2},{1,3},{2,4},{3,5},{4,6},{5,7},{6,0},{7,1},{8,10},{9,11},{10,... | collective-permute-start | bytes 786440 | tf_op jit(solution)/shard_map/ppermute | solution.py:30
  123.2 60.9 %collective-permute-start.9 = (f32[4,128,1024]{2,1,0:T(8,128)S(1)}, f32[4,128,1024]{2,1,0:T(8,128)S(1)}, u32[]{:S(2)}, u32[]{:S(2)}) collective-permute-start(f32[4,128,1024]{2,1,0:T(8,128)S(1)} %pad_maximum_fusion.own), channel_id=1, source_target_pairs={{0,1},{1,0},{2,3},{3,2},{4,5},{5,4},{6,7},{7,6},{8,9},{9,8},{10,11... | collective-permute-start | bytes 6291464 | tf_op jit(solution)/shard_map/ppermute | solution.py:30
  123.4 17.4 %collective-permute-start.23 = (f32[4,2,64,256]{3,2,1,0:T(8,128)S(1)}, f32[4,2,64,256]{3,2,1,0:T(8,128)S(1)}, u32[]{:S(2)}, u32[]{:S(2)}) collective-permute-start(f32[4,2,64,256]{3,2,1,0:T(8,128)S(1)} %pad_maximum_fusion.2.refs_4_.refs_20_), channel_id=1, source_target_pairs={{0,16},{1,17},{2,18},{3,19},{4,20},{5,21},{6,22},{7,23},{8,24},{9,... | collective-permute-start | bytes 1572872 | tf_op jit(solution)/shard_map/ppermute | solution.py:30
  126.7 15.5 %collective-permute-start.32 = (f32[4,2,64,256]{3,2,1,0:T(8,128)S(1)}, f32[4,2,64,256]{3,2,1,0:T(8,128)S(1)}, u32[]{:S(2)}, u32[]{:S(2)}) collective-permute-start(f32[4,2,64,256]{3,2,1,0:T(8,128)S(1)} %collective-permute-done.30.refs_12_.refs_28_), channel_id=1, source_target_pairs={{0,112},{1,113},{2,114},{3,115},{4,116},{5,117},{6,118},{7,119},{8... | collective-permute-start | bytes 1572872 | tf_op jit(solution)/shard_map/ppermute | solution.py:30
  128.5 60.1 %collective-permute-start.19 = (f32[4,128,1024]{2,1,0:T(8,128)S(1)}, f32[4,128,1024]{2,1,0:T(8,128)S(1)}, u32[]{:S(2)}, u32[]{:S(2)}) collective-permute-start(f32[4,128,1024]{2,1,0:T(8,128)S(1)} %pad_maximum_fusion.1.own), channel_id=1, source_target_pairs={{0,1},{1,0},{2,3},{3,2},{4,5},{5,4},{6,7},{7,6},{8,9},{9,8},{10,11... | collective-permute-start | bytes 6291464 | tf_op jit(solution)/shard_map/ppermute | solution.py:30
  128.7 23.4 %collective-permute-start.31 = (f32[4,2,64,256]{3,2,1,0:T(8,128)S(1)}, f32[4,2,64,256]{3,2,1,0:T(8,128)S(1)}, u32[]{:S(2)}, u32[]{:S(2)}) collective-permute-start(f32[4,2,64,256]{3,2,1,0:T(8,128)S(1)} %collective-permute-done.30.refs_12_.refs_28_), channel_id=1, source_target_pairs={{0,16},{1,17},{2,18},{3,19},{4,20},{5,21},{6,22},{7,23},{8,24},{9,... | collective-permute-start | bytes 1572872 | tf_op jit(solution)/shard_map/ppermute | solution.py:30
  140.8 12.7 %collective-permute-start.26 = (f32[4,2,64,256]{3,2,1,0:T(8,128)S(1)}, f32[4,2,64,256]{3,2,1,0:T(8,128)S(1)}, u32[]{:S(2)}, u32[]{:S(2)}) collective-permute-start(f32[4,2,64,256]{3,2,1,0:T(8,128)S(1)} %collective-permute-done.24.refs_6_.refs_22_), channel_id=1, source_target_pairs={{0,112},{1,113},{2,114},{3,115},{4,116},{5,117},{6,118},{7,119},{8... | collective-permute-start | bytes 1572872 | tf_op jit(solution)/shard_map/ppermute | solution.py:30
  142.3 21.0 %collective-permute-start.25 = (f32[4,2,64,256]{3,2,1,0:T(8,128)S(1)}, f32[4,2,64,256]{3,2,1,0:T(8,128)S(1)}, u32[]{:S(2)}, u32[]{:S(2)}) collective-permute-start(f32[4,2,64,256]{3,2,1,0:T(8,128)S(1)} %collective-permute-done.23.refs_5_.refs_21_), channel_id=1, source_target_pairs={{0,16},{1,17},{2,18},{3,19},{4,20},{5,21},{6,22},{7,23},{8,24},{9,... | collective-permute-start | bytes 1572872 | tf_op jit(solution)/shard_map/ppermute | solution.py:30
  152.0 12.1 %collective-permute-start.34 = (f32[4,2,64,256]{3,2,1,0:T(8,128)S(1)}, f32[4,2,64,256]{3,2,1,0:T(8,128)S(1)}, u32[]{:S(2)}, u32[]{:S(2)}) collective-permute-start(f32[4,2,64,256]{3,2,1,0:T(8,128)S(1)} %collective-permute-done.32.refs_14_.refs_30_), channel_id=1, source_target_pairs={{0,112},{1,113},{2,114},{3,115},{4,116},{5,117},{6,118},{7,119},{8... | collective-permute-start | bytes 1572872 | tf_op jit(solution)/shard_map/ppermute | solution.py:30
  153.5 21.0 %collective-permute-start.33 = (f32[4,2,64,256]{3,2,1,0:T(8,128)S(1)}, f32[4,2,64,256]{3,2,1,0:T(8,128)S(1)}, u32[]{:S(2)}, u32[]{:S(2)}) collective-permute-start(f32[4,2,64,256]{3,2,1,0:T(8,128)S(1)} %collective-permute-done.31.refs_13_.refs_29_), channel_id=1, source_target_pairs={{0,16},{1,17},{2,18},{3,19},{4,20},{5,21},{6,22},{7,23},{8,24},{9,... | collective-permute-start | bytes 1572872 | tf_op jit(solution)/shard_map/ppermute | solution.py:30
  163.3 20.8 %collective-permute-start.27 = (f32[4,2,64,256]{3,2,1,0:T(8,128)S(1)}, f32[4,2,64,256]{3,2,1,0:T(8,128)S(1)}, u32[]{:S(2)}, u32[]{:S(2)}) collective-permute-start(f32[4,2,64,256]{3,2,1,0:T(8,128)S(1)} %collective-permute-done.25.refs_7_.refs_23_), channel_id=1, source_target_pairs={{0,16},{1,17},{2,18},{3,19},{4,20},{5,21},{6,22},{7,23},{8,24},{9,... | collective-permute-start | bytes 1572872 | tf_op jit(solution)/shard_map/ppermute | solution.py:30
  164.2 20.0 %collective-permute-start.36 = (f32[4,2,64,256]{3,2,1,0:T(8,128)S(1)}, f32[4,2,64,256]{3,2,1,0:T(8,128)S(1)}, u32[]{:S(2)}, u32[]{:S(2)}) collective-permute-start(f32[4,2,64,256]{3,2,1,0:T(8,128)S(1)} %collective-permute-done.34.refs_16_.refs_32_), channel_id=1, source_target_pairs={{0,112},{1,113},{2,114},{3,115},{4,116},{5,117},{6,118},{7,119},{8... | collective-permute-start | bytes 1572872 | tf_op jit(solution)/shard_map/ppermute | solution.py:30
  174.5 15.9 %collective-permute-start.28 = (f32[4,2,64,256]{3,2,1,0:T(8,128)S(1)}, f32[4,2,64,256]{3,2,1,0:T(8,128)S(1)}, u32[]{:S(2)}, u32[]{:S(2)}) collective-permute-start(f32[4,2,64,256]{3,2,1,0:T(8,128)S(1)} %collective-permute-done.26.refs_8_.refs_24_), channel_id=1, source_target_pairs={{0,112},{1,113},{2,114},{3,115},{4,116},{5,117},{6,118},{7,119},{8... | collective-permute-start | bytes 1572872 | tf_op jit(solution)/shard_map/ppermute | solution.py:30
  184.1 15.2 %collective-permute-start.35 = (f32[4,2,64,256]{3,2,1,0:T(8,128)S(1)}, f32[4,2,64,256]{3,2,1,0:T(8,128)S(1)}, u32[]{:S(2)}, u32[]{:S(2)}) collective-permute-start(f32[4,2,64,256]{3,2,1,0:T(8,128)S(1)} %collective-permute-done.33.refs_15_.refs_31_), channel_id=1, source_target_pairs={{0,16},{1,17},{2,18},{3,19},{4,20},{5,21},{6,22},{7,23},{8,24},{9,... | collective-permute-start | bytes 1572872 | tf_op jit(solution)/shard_map/ppermute | solution.py:30
  184.1 26.0 %collective-permute-start.29 = (f32[4,2,64,256]{3,2,1,0:T(8,128)S(1)}, f32[4,2,64,256]{3,2,1,0:T(8,128)S(1)}, u32[]{:S(2)}, u32[]{:S(2)}) collective-permute-start(f32[4,2,64,256]{3,2,1,0:T(8,128)S(1)} %collective-permute-done.27.refs_9_.refs_25_), channel_id=1, source_target_pairs={{0,16},{1,17},{2,18},{3,19},{4,20},{5,21},{6,22},{7,23},{8,24},{9,... | collective-permute-start | bytes 1572872 | tf_op jit(solution)/shard_map/ppermute | solution.py:30
  184.1 26.0 %collective-permute-start.37 = (f32[4,2,64,256]{3,2,1,0:T(8,128)S(1)}, f32[4,2,64,256]{3,2,1,0:T(8,128)S(1)}, u32[]{:S(2)}, u32[]{:S(2)}) collective-permute-start(f32[4,2,64,256]{3,2,1,0:T(8,128)S(1)} %collective-permute-done.36.refs_18_.refs_34_), channel_id=1, source_target_pairs={{0,112},{1,113},{2,114},{3,115},{4,116},{5,117},{6,118},{7,119},{8... | collective-permute-start | bytes 1572872 | tf_op jit(solution)/shard_map/ppermute | solution.py:30
  218.8 76.0 %collective-permute-start.46 = (f32[1024,256]{1,0:T(8,128)S(1)}, f32[1024,256]{1,0:T(8,128)}, u32[]{:S(2)}, u32[]{:S(2)}) collective-permute-start(f32[1024,256]{1,0:T(8,128)S(1)} %get-tuple-element.36), channel_id=1, source_target_pairs={{0,96},{1,112},{2,66},{3,82},{4,36},{5,52},{6,6},{7,22},{8,224},{9... | collective-permute-start | bytes 3145736 | tf_op jit(solution)/shard_map/ppermute | solution.py:30
  220.9 75.7 %collective-permute-start.39 = (f32[1024,256]{1,0:T(8,128)S(1)}, f32[1024,256]{1,0:T(8,128)S(1)}, u32[]{:S(2)}, u32[]{:S(2)}) collective-permute-start(f32[1024,256]{1,0:T(8,128)S(1)} %get-tuple-element.36), channel_id=1, source_target_pairs={{0,6},{1,7},{2,4},{3,5},{4,2},{5,3},{6,0},{7,1},{8,14},{9,15},{10,... | collective-permute-start | bytes 3145736 | tf_op jit(solution)/shard_map/ppermute | solution.py:30
  222.9 75.6 %collective-permute-start.48 = (f32[1024,256]{1,0:T(8,128)S(1)}, f32[1024,256]{1,0:T(8,128)}, u32[]{:S(2)}, u32[]{:S(2)}) collective-permute-start(f32[1024,256]{1,0:T(8,128)S(1)} %get-tuple-element.38), channel_id=1, source_target_pairs={{0,32},{1,48},{2,2},{3,18},{4,100},{5,116},{6,70},{7,86},{8,40},{9... | collective-permute-start | bytes 3145736 | tf_op jit(solution)/shard_map/ppermute | solution.py:30
  237.6 77.3 %collective-permute-start.42 = (f32[1024,256]{1,0:T(8,128)S(1)}, f32[1024,256]{1,0:T(8,128)}, u32[]{:S(2)}, u32[]{:S(2)}) collective-permute-start(f32[1024,256]{1,0:T(8,128)S(1)} %get-tuple-element.35), channel_id=1, source_target_pairs={{0,0},{1,16},{2,98},{3,114},{4,68},{5,84},{6,38},{7,54},{8,128},{9... | collective-permute-start | bytes 3145736 | tf_op jit(solution)/shard_map/ppermute | solution.py:30
  239.5 84.8 %collective-permute-start.44 = (f32[1024,256]{1,0:T(8,128)}, f32[1024,256]{1,0:T(8,128)}, u32[]{:S(2)}, u32[]{:S(2)}) collective-permute-start(f32[1024,256]{1,0:T(8,128)} %get-tuple-element.37), channel_id=1, source_target_pairs={{0,64},{1,80},{2,34},{3,50},{4,4},{5,20},{6,102},{7,118},{8,192},{... | collective-permute-start | bytes 3145736 | tf_op jit(solution)/shard_map/ppermute | solution.py:30
  294.7 42.2 %collective-permute-start.41 = (f32[1024,256]{1,0:T(8,128)S(1)}, f32[1024,256]{1,0:T(8,128)S(1)}, u32[]{:S(2)}, u32[]{:S(2)}) collective-permute-start(f32[1024,256]{1,0:T(8,128)S(1)} %get-tuple-element.38), channel_id=1, source_target_pairs={{0,2},{1,3},{2,0},{3,1},{4,6},{5,7},{6,4},{7,5},{8,10},{9,11},{10,... | collective-permute-start | bytes 3145736 | tf_op jit(solution)/shard_map/ppermute | solution.py:30
  296.6 42.2 %collective-permute-start.38 = (f32[1024,256]{1,0:T(8,128)S(1)}, f32[1024,256]{1,0:T(8,128)S(1)}, u32[]{:S(2)}, u32[]{:S(2)}) collective-permute-start(f32[1024,256]{1,0:T(8,128)S(1)} %get-tuple-element.35), channel_id=1, source_target_pairs={{0,0},{1,1},{2,6},{3,7},{4,4},{5,5},{6,2},{7,3},{8,8},{9,9},{10,14... | collective-permute-start | bytes 3145736 | tf_op jit(solution)/shard_map/ppermute | solution.py:30
  298.6 49.9 %collective-permute-start.40 = (f32[1024,256]{1,0:T(8,128)}, f32[1024,256]{1,0:T(8,128)}, u32[]{:S(2)}, u32[]{:S(2)}) collective-permute-start(f32[1024,256]{1,0:T(8,128)} %get-tuple-element.37), channel_id=1, source_target_pairs={{0,4},{1,5},{2,2},{3,3},{4,0},{5,1},{6,6},{7,7},{8,12},{9,13},{10,... | collective-permute-start | bytes 3145736 | tf_op jit(solution)/shard_map/ppermute | solution.py:30
  314.9 43.8 %collective-permute-start.43 = (f32[1024,256]{1,0:T(8,128)}, f32[1024,256]{1,0:T(8,128)}, u32[]{:S(2)}, u32[]{:S(2)}) collective-permute-start(f32[1024,256]{1,0:T(8,128)} %collective-permute-done.42), channel_id=1, source_target_pairs={{0,0},{1,1},{2,2},{3,3},{4,4},{5,5},{6,6},{7,7},{8,8},{9,9},{10,10... | collective-permute-start | bytes 3145736 | tf_op jit(solution)/shard_map/ppermute | solution.py:30
  324.4 61.4 %collective-permute-start.45 = (f32[1024,256]{1,0:T(8,128)}, f32[1024,256]{1,0:T(8,128)}, u32[]{:S(2)}, u32[]{:S(2)}) collective-permute-start(f32[1024,256]{1,0:T(8,128)} %collective-permute-done.44), channel_id=1, source_target_pairs={{0,4},{1,5},{2,6},{3,7},{4,0},{5,1},{6,2},{7,3},{8,12},{9,13},{10,... | collective-permute-start | bytes 3145736 | tf_op jit(solution)/shard_map/ppermute | solution.py:30
  336.9 55.3 %collective-permute-start.47 = (f32[1024,256]{1,0:T(8,128)}, f32[1024,256]{1,0:T(8,128)}, u32[]{:S(2)}, u32[]{:S(2)}) collective-permute-start(f32[1024,256]{1,0:T(8,128)} %collective-permute-done.46), channel_id=1, source_target_pairs={{0,2},{1,3},{2,4},{3,5},{4,6},{5,7},{6,0},{7,1},{8,10},{9,11},{10,... | collective-permute-start | bytes 3145736 | tf_op jit(solution)/shard_map/ppermute | solution.py:30
  339.8 58.7 %collective-permute-start.49 = (f32[1024,256]{1,0:T(8,128)}, f32[1024,256]{1,0:T(8,128)}, u32[]{:S(2)}, u32[]{:S(2)}) collective-permute-start(f32[1024,256]{1,0:T(8,128)} %collective-permute-done.48), channel_id=1, source_target_pairs={{0,6},{1,7},{2,0},{3,1},{4,2},{5,3},{6,4},{7,5},{8,134},{9,135},{1... | collective-permute-start | bytes 3145736 | tf_op jit(solution)/shard_map/ppermute | solution.py:30
  (12 other events, 526.0 us)
